TPU v7x, 128 devices: a whole 4x4x4 slice. The times are simulated.
128 devices in a mesh: section: 16 (over z_hi, y, core), seq: 8 (over x, z_lo).
Axes of the slice: x: 4, y: 4, z: 4 (z_hi: 2, z_lo: 2; z = z_hi * 2 + z_lo), core: 2. Of those that a mesh axis runs over, the one named last changes fastest.
Arguments:
- forward_rows: bfloat16 [16, 1024, 4096], P('section', 'seq'), may hold values from -54 to 54
- saved_rows: bfloat16 [16, 1024, 4096], P('section', 'seq'), may hold values from -54 to 54
- output_grad: bfloat16 [16, 1024, 4096], P('section', 'seq'), may hold values from -6 to 6
- forward_docs: int32 [16, 1024], replicated, may hold values from 0 to 3, never falling along the last dimension, each value on 1 to 512 neighbouring positions
- backward_docs: int32 [16, 1024], replicated, may hold values from 0 to 3, never falling along the last dimension, each value on 1 to 512 neighbouring positions
- norm_gain: float32 [16, 4096], P('section'), may hold values from 0.7 to 8
- query_weight: bfloat16 [16, 4096, 4096], P('section', None, 'seq'), may hold values from -0.09375 to 0.09375
- key_matrix: bfloat16 [16, 4096, 1024], P('section', None, 'seq'), may hold values from -0.09375 to 0.09375
- value_matrix: bfloat16 [16, 4096, 1024], P('section', None, 'seq'), may hold values from -0.09375 to 0.09375
Outputs:
- section_output: bfloat16 [16, 1024, 4096], P('section', 'seq')
- input_grad: bfloat16 [16, 1024, 4096], P('section', 'seq')
Inputs may be any that keep to these rules, and one draw needn't show every extreme that they name: `forward_docs`: document ids never fall along a row; every document holds at most 512 tokens and some document of each row holds exactly that many. `backward_docs`: document ids never fall along a row; every document holds at most 512 tokens and some document of each row holds exactly that many.
All inputs are finite; a program needn't handle non-finite values.
Results may differ from a plain program's by a relative error of at most 0.017.
The roundings to bfloat16 on the way count: a program that leaves them out, or rounds other values in their place, can miss the bound.
Values may be sent and summed in bfloat16 or wider, within the bound.
A program may use at most 192 MiB of HBM per device.

v0:
```python
import jax
import jax.numpy as jnp
from jax import lax
from jax.sharding import PartitionSpec as P

MODEL_WIDTH = 4096
HEAD_SIZE = 128


epsilon = 1e-05
rope_base = 500000.0


def passed_along(shard, axis, by):
    peers = lax.axis_size(axis)
    pairs = [(i, i + by) for i in range(peers) if 0 <= i + by < peers]
    return lax.ppermute(shard, axis, pairs)


def rotation_tables(positions):
    half = HEAD_SIZE // 2
    freqs = rope_base ** (-(jnp.arange(half, dtype=jnp.float32) * 2.0 / HEAD_SIZE))
    angles = positions[:, None] * freqs[None, :]
    return (jnp.cos(angles), jnp.sin(angles))


def rotate(values, cosines, sines, sign):
    half = values.shape[-1] // 2
    extra = (1,) * (values.ndim - 2)
    cos_wide = cosines.reshape(cosines.shape[:1] + extra + cosines.shape[1:])
    sin_wide = sines.reshape(sines.shape[:1] + extra + sines.shape[1:])
    first = values[..., :half]
    second = values[..., half:]
    return jnp.concatenate(
        [first * cos_wide - sign * second * sin_wide, second * cos_wide + sign * first * sin_wide],
        axis=-1,
    )


def pair_mask(row_docs, col_docs, row_begin):
    row_pos = row_begin + lax.iota(jnp.int32, row_docs.shape[0])
    col_pos = lax.iota(jnp.int32, col_docs.shape[0])
    return (col_pos[None, :] <= row_pos[:, None]) & (row_docs[:, None] == col_docs[None, :])


def block_probs(query_block, key_heads, allowed):
    scores = jnp.einsum(
        "tjgd,sjd->jgts", query_block, key_heads, preferred_element_type=jnp.float32
    ) * HEAD_SIZE ** (-0.5)
    scores = jnp.where(allowed, scores, -1e30)
    row_top = jnp.max(scores, axis=-1, keepdims=True)
    exp_scores = jnp.where(allowed, jnp.exp(scores - row_top), 0.0)
    return exp_scores / jnp.sum(exp_scores, axis=-1, keepdims=True)


def attend(query_rows_local, key_rows, value_rows, documents):
    sequence_length = query_rows_local.shape[0]
    groups = key_rows.shape[1] // HEAD_SIZE
    group_size = query_rows_local.shape[1] // key_rows.shape[1]
    query_head_count = query_rows_local.reshape(sequence_length, groups, group_size, HEAD_SIZE)
    key_heads = key_rows.reshape(sequence_length, groups, HEAD_SIZE)
    value_heads = value_rows.reshape(sequence_length, groups, HEAD_SIZE)
    block_rows = min(512, sequence_length)
    pieces = []
    for block_index in range(sequence_length // block_rows):
        begin_row = block_index * block_rows
        end_row = begin_row + block_rows
        allowed = pair_mask(documents[begin_row:end_row], documents[:end_row], begin_row)
        probability = block_probs(
            query_head_count[begin_row:end_row], key_heads[:end_row], allowed
        ).astype(jnp.bfloat16)
        mixed_rows = jnp.einsum(
            "jgts,sjd->tjgd", probability, value_heads[:end_row], preferred_element_type=jnp.float32
        )
        pieces.append(mixed_rows.astype(jnp.bfloat16))
    return lax.optimization_barrier(
        jnp.concatenate(pieces, 0).reshape(sequence_length, query_rows_local.shape[1])
    )


def attend_back(query_rows_local, key_rows, value_rows, output_gradient, documents, cosines, sines):
    sequence_length = query_rows_local.shape[0]
    groups = key_rows.shape[1] // HEAD_SIZE
    group_size = query_rows_local.shape[1] // key_rows.shape[1]
    query_head_count = query_rows_local.reshape(sequence_length, groups, group_size, HEAD_SIZE)
    key_heads = key_rows.reshape(sequence_length, groups, HEAD_SIZE)
    value_heads = value_rows.reshape(sequence_length, groups, HEAD_SIZE)
    head_gradients = output_gradient.reshape(sequence_length, groups, group_size, HEAD_SIZE)
    scale = HEAD_SIZE ** (-0.5)
    key_grad = jnp.zeros((sequence_length, groups, HEAD_SIZE), jnp.float32)
    value_grad = jnp.zeros((sequence_length, groups, HEAD_SIZE), jnp.float32)
    block_rows = min(512, sequence_length)
    query_pieces = []
    for block_index in range(sequence_length // block_rows):
        begin_row = block_index * block_rows
        end_row = begin_row + block_rows
        allowed = pair_mask(documents[begin_row:end_row], documents[:end_row], begin_row)
        query_block = query_head_count[begin_row:end_row]
        grad_block = head_gradients[begin_row:end_row]
        probability = block_probs(query_block, key_heads[:end_row], allowed)
        grad_probs = jnp.einsum(
            "tjgd,sjd->jgts", grad_block, value_heads[:end_row], preferred_element_type=jnp.float32
        )
        row_delta = jnp.sum(probability * grad_probs, axis=-1, keepdims=True)
        grad_scores = (probability * (grad_probs - row_delta)).astype(jnp.bfloat16)
        query_piece = (
            jnp.einsum(
                "jgts,sjd->tjgd",
                grad_scores,
                key_heads[:end_row],
                preferred_element_type=jnp.float32,
            )
            * scale
        )
        query_piece = rotate(
            query_piece, cosines[begin_row:end_row], sines[begin_row:end_row], -1.0
        )
        query_pieces.append(query_piece.astype(jnp.bfloat16))
        key_grad = key_grad.at[:end_row].add(
            jnp.einsum(
                "jgts,tjgd->sjd", grad_scores, query_block, preferred_element_type=jnp.float32
            )
            * scale
        )
        value_grad = value_grad.at[:end_row].add(
            jnp.einsum(
                "jgts,tjgd->sjd",
                probability.astype(jnp.bfloat16),
                grad_block,
                preferred_element_type=jnp.float32,
            )
        )
    query_grad = jnp.concatenate(query_pieces, 0).reshape(
        sequence_length, query_rows_local.shape[1]
    )
    key_grad = (
        rotate(key_grad, cosines, sines, -1.0)
        .astype(jnp.bfloat16)
        .reshape(sequence_length, groups * HEAD_SIZE)
    )
    value_grad = value_grad.astype(jnp.bfloat16).reshape(sequence_length, groups * HEAD_SIZE)
    return lax.optimization_barrier((query_grad, key_grad, value_grad))


def token_scale(hidden):
    return lax.rsqrt(jnp.mean(hidden * hidden, axis=-1, keepdims=True) + epsilon)


def heads_inputs(rows_whole, weights):
    query_weight, key_matrix, value_matrix = weights
    sequence_length = rows_whole.shape[0]
    cosines, sines = rotation_tables(jnp.arange(sequence_length, dtype=jnp.float32))
    query_proj = jnp.dot(rows_whole, query_weight, preferred_element_type=jnp.float32)
    key_projected_rows = jnp.dot(rows_whole, key_matrix, preferred_element_type=jnp.float32)
    value_projected_rows = jnp.dot(rows_whole, value_matrix, preferred_element_type=jnp.float32)
    query_rows_local = (
        rotate(query_proj.reshape(sequence_length, -1, HEAD_SIZE), cosines, sines, 1.0)
        .reshape(sequence_length, -1)
        .astype(jnp.bfloat16)
    )
    key_rows = (
        rotate(key_projected_rows.reshape(sequence_length, -1, HEAD_SIZE), cosines, sines, 1.0)
        .reshape(sequence_length, -1)
        .astype(jnp.bfloat16)
    )
    value_rows = value_projected_rows.astype(jnp.bfloat16)
    return (query_rows_local, key_rows, value_rows, cosines, sines)


def body(
    forward_rows,
    saved_rows,
    output_grad,
    forward_docs,
    backward_docs,
    norm_gain,
    query_weight,
    key_matrix,
    value_matrix,
):
    section_index = lax.axis_index("section")
    first_docs = lax.dynamic_index_in_dim(forward_docs, section_index, 0, keepdims=False)
    back_docs = lax.dynamic_index_in_dim(backward_docs, section_index, 0, keepdims=False)
    gain_row = norm_gain[0]
    weights = (query_weight[0], key_matrix[0], value_matrix[0])
    forward_hidden = forward_rows[0].astype(jnp.float32)
    forward_normed = (forward_hidden * token_scale(forward_hidden) * gain_row).astype(jnp.bfloat16)
    back_hidden = saved_rows[0].astype(jnp.float32)
    back_scale = token_scale(back_hidden)
    back_normed = (back_hidden * back_scale * gain_row).astype(jnp.bfloat16)
    forward_whole = lax.all_gather(forward_normed, "seq", axis=0, tiled=True)
    query_rows_local, key_rows, value_rows, cosines, sines = heads_inputs(forward_whole, weights)
    mixed_rows = attend(query_rows_local, key_rows, value_rows, first_docs)
    mixed_rows = lax.all_to_all(mixed_rows, "seq", split_axis=0, concat_axis=1, tiled=True)
    first_out = (forward_hidden + mixed_rows.astype(jnp.float32)).astype(jnp.bfloat16)
    section_output = passed_along(first_out, "section", 1)
    back_whole = lax.all_gather(back_normed, "seq", axis=0, tiled=True)
    head_gradients = lax.all_to_all(output_grad[0], "seq", split_axis=1, concat_axis=0, tiled=True)
    query_rows_local, key_rows, value_rows, cosines, sines = heads_inputs(back_whole, weights)
    query_grad, key_grad, value_grad = attend_back(
        query_rows_local, key_rows, value_rows, head_gradients, back_docs, cosines, sines
    )
    term = jnp.einsum("tc,rc->tr", query_grad, weights[0], preferred_element_type=jnp.float32)
    term = term + jnp.einsum("tc,rc->tr", key_grad, weights[1], preferred_element_type=jnp.float32)
    input_sum = lax.psum_scatter(
        (
            term
            + jnp.einsum("tc,rc->tr", value_grad, weights[2], preferred_element_type=jnp.float32)
        ).astype(jnp.bfloat16),
        "seq",
        scatter_dimension=0,
        tiled=True,
    ).astype(jnp.float32)
    gained = gain_row * input_sum
    inner_sum = jnp.sum(back_hidden * gained, axis=-1, keepdims=True)
    norm_part = (
        back_scale * gained
        - back_hidden * (back_scale * back_scale * back_scale) * inner_sum / MODEL_WIDTH
    )
    first_grad = (output_grad[0].astype(jnp.float32) + norm_part).astype(jnp.bfloat16)
    input_grad = passed_along(first_grad, "section", -1)
    return (section_output[None], input_grad[None])


def solution(mesh):
    placed = (
        P("section", "seq", None),
        P("section", "seq", None),
        P("section", "seq", None),
        P(),
        P(),
        P("section", None),
        P("section", None, "seq"),
        P("section", None, "seq"),
        P("section", None, "seq"),
    )
    return jax.shard_map(
        body,
        mesh=mesh,
        in_specs=placed,
        out_specs=(P("section", "seq", None), P("section", "seq", None)),
        check_vma=False,
    )
```

profile of v0, /device:TPU:25, one launch (start us, length us, event | category | flops | bytes accessed | tf_op | source)
XLA Modules:
  0.0 669.3 jit_solution(13444456036712751143)
XLA Ops:
  11.5 3.5 fusion.35
  17.6 5.4 all-to-all-start.1
  23.5 6.4 copy.76
  35.3 6.1 all-to-all-done.1
  46.4 148.5 %all-gather.5.cloned.1.call-done = bf16[1024,4096]{1,0:T(8,128)(2,1)} async-done(((bf16[128,4096]{1,0:T(8,128)(2,1)}), bf16[1024,4096]{1,0:T(8,128)(2,1)}) %all-gather.5.cloned.1.call-update) | async-done | bytes 8388624 | tf_op jit(solution)/shard_map/all_gather | solution.py:197
  194.9 6.4 convolution_bitcast_fusion
  202.5 5.8 fusion.3
  208.3 163.0 %all-gather.3.cloned.1.call-done = bf16[1024,4096]{1,0:T(8,128)(2,1)} async-done(((bf16[128,4096]{1,0:T(8,128)(2,1)}), bf16[1024,4096]{1,0:T(8,128)(2,1)}) %all-gather.3.cloned.1.call-update) | async-done | bytes 8388624 | tf_op jit(solution)/shard_map/all_gather | solution.py:191
  371.3 8.5 %fusion.5 = f32[1024,4,128]{0,2,1:T(8,128)S(1)} fusion(bf16[4,128,4096]{2,1,0:T(8,128)(2,1)} %bitcast.349, bf16[1024,4096]{1,0:T(8,128)(2,1)} %all-gather.3.cloned.1.call-done), kind=kOutput, calls=%fused_computation.10 | convolution fusion | flops 4294967296 | bytes 14680064 | tf_op jit(solution)/shard_map/dot_general | solution.py:153
  386.3 2.3 convolution_convert_fusion
  397.2 5.2 fusion
  402.4 2.6 fusion.78
  405.1 5.1 fusion.12
  412.7 2.9 convolution_bitcast_fusion.1
  417.8 8.6 %fusion.20 = f32[1024,4096]{1,0:T(8,128)} fusion(bf16[1024,512]{0,1:T(8,128)(2,1)S(1)} %pad_maximum_fusion.1, bf16[1,4096,512]{2,1,0:T(8,128)(2,1)S(1)} %copy-done.6), kind=kOutput, calls=%fused_computation.32 | convolution fusion | flops 4294967296 | bytes 22020096 | tf_op jit(solution)/shard_map/tc,rc->tr/dot_general | solution.py:203
  426.4 8.1 %fusion.86 = f32[1024,4096]{1,0:T(8,128)} fusion(bf16[1024,128]{0,1:T(8,128)(2,1)S(1)} %pad_maximum_fusion.7, bf16[1,4096,128]{2,1,0:T(8,128)(2,1)S(1)} %copy-done), kind=kOutput, calls=%fused_computation.105 | convolution fusion | flops 1073741824 | bytes 18087936 | tf_op jit(solution)/shard_map/tc,rc->tr/dot_general | solution.py:204
  434.5 15.3 %add_convert_fusion = bf16[1024,4096]{1,0:T(8,128)(2,1)} fusion(f32[1024,4096]{1,0:T(8,128)} %fusion.20, f32[1024,4096]{1,0:T(8,128)} %fusion.86, bf16[1024,128]{1,0:T(8,128)(2,1)S(1)} %fusion.78, bf16[1,4096,128]{2,1,0:T(8,128)(2,1)S(1)} %copy-done.11), kind=kOutput, calls=%fused_computation | convolution fusion | flops 1086324736 | bytes 43253760 | tf_op jit(solution)/shard_map/tc,rc->tr/dot_general | solution.py:208
  454.8 2.3 convolution_convert_fusion.1
  461.0 2.9 fusion.60
  464.6 29.1 %all_to_all.29 = bf16[8,128,512]{2,1,0:T(8,128)(2,1)S(1)} all-to-all(bf16[8,128,512]{2,1,0:T(8,128)(2,1)S(1)} %bitcast.353), channel_id=1, replica_groups=mesh['section'=16,'seq'=8] {'seq'}, dimensions={0} | all-to-all | bytes 2097152 | tf_op jit(solution)/shard_map/all_to_all | solution.py:194
  496.1 4.6 collective-permute-start
  500.8 135.1 %reduce-scatter.2.cloned.1.call-done = bf16[128,4096]{1,0:T(8,128)(2,1)} async-done(((bf16[1024,4096]{1,0:T(8,128)(2,1)}), bf16[128,4096]{1,0:T(8,128)(2,1)}) %reduce-scatter.2.cloned.1.call-update) | async-done | bytes 1048592 | tf_op jit(solution)/shard_map/reduce_scatter | solution.py:205
  639.6 2.5 collective-permute-start.1
  642.2 17.2 %collective-permute-done.1 = bf16[128,4096]{1,0:T(8,128)(2,1)S(1)} collective-permute-done((bf16[128,4096]{1,0:T(8,128)(2,1)S(1)}, bf16[128,4096]{1,0:T(8,128)(2,1)S(1)}, u32[]{:S(2)}, u32[]{:S(2)}) %collective-permute-start.1) | collective-permute-done | bytes 1048608 | tf_op jit(solution)/shard_map/ppermute | solution.py:17
  (119 shorter events, 57.3 us)
Async XLA Ops:
  7.2 187.7 %copy-start = (bf16[1,4096,128]{2,1,0:T(8,128)(2,1)S(1)}, bf16[1,4096,128]{2,1,0:T(8,128)(2,1)}, u32[]{:S(2)}) copy-start(bf16[1,4096,128]{2,1,0:T(8,128)(2,1)} %param.28) | copy-start | bytes 3145732
  7.2 8.6 %copy-start.4 = (bf16[1,128,4096]{2,1,0:T(8,128)(2,1)S(1)}, bf16[1,128,4096]{2,1,0:T(8,128)(2,1)}, u32[]{:S(2)}) copy-start(bf16[1,128,4096]{2,1,0:T(8,128)(2,1)} %param.23) | copy-start | bytes 3145732
  7.2 187.7 %all-gather.5.cloned.1.call-start = ((), (), s32[]{:S(2)}) async-start(), calls=%async_computation.4 | async-start | bytes 9437184 | tf_op jit(solution)/shard_map/all_gather | solution.py:197
  15.0 356.3 %all-gather.3.cloned.1.call-start = ((), (), s32[]{:S(2)}) async-start(), calls=%async_computation.3 | async-start | bytes 9437184 | tf_op jit(solution)/shard_map/all_gather | solution.py:191
  17.6 23.8 %all-to-all-start.1 = ((bf16[128,8,512]{2,0,1:T(8,128)(2,1)}), bf16[128,8,512]{2,0,1:T(8,128)(2,1)S(1)}, u32[]{:S(2)}, u32[]{:S(2)}) async-start(bf16[128,8,512]{2,0,1:T(8,128)(2,1)} %copy.43), calls=%async_computation.1 | async-start | bytes 2097152 | tf_op jit(solution)/shard_map/all_to_all | solution.py:198
  22.9 612.9 %reduce-scatter.2.cloned.1.call-start = ((), (), s32[]{:S(2)}) async-start(), calls=%async_computation.5 | async-start | bytes 9437184 | tf_op jit(solution)/shard_map/reduce_scatter | solution.py:205
  194.9 7.6 %copy-start.1 = (bf16[1024,4096]{1,0:T(8,128)(2,1)S(1)}, bf16[1024,4096]{1,0:T(8,128)(2,1)}, u32[]{:S(2)}) copy-start(bf16[1024,4096]{1,0:T(8,128)(2,1)} %all-gather.5.cloned.1.call-done) | copy-start | bytes 25165828
  194.9 7.6 %copy-start.7 = (bf16[512,4096]{1,0:T(8,128)(2,1)S(1)}, bf16[512,4096]{1,0:T(8,128)(2,1)}, u32[]{:S(2)}) copy-start(bf16[512,4096]{1,0:T(8,128)(2,1)} %copy.76) | copy-start | bytes 12582916
  371.3 8.5 %copy-start.9 = (f32[1024,4,128]{0,2,1:T(8,128)S(1)}, f32[1024,4,128]{0,2,1:T(8,128)}, u32[]{:S(2)}) copy-start(f32[1024,4,128]{0,2,1:T(8,128)} %fusion.3) | copy-start | bytes 6291460
  383.5 2.6 slice-start.5
  383.5 2.8 copy-start.10
  397.2 15.5 %slice-start = ((s8[8388608]{0:T(1024)(128)(4,1)}), s8[4194304]{0:T(1024)(128)(4,1)S(1)}, s32[]{:S(2)}) async-start(s8[8388608]{0:T(1024)(128)(4,1)} %bitcast.340), calls=%async_computation.6 | async-start | bytes 8388608
  402.4 10.3 %slice-start.1 = ((s8[8388608]{0:T(1024)(128)(4,1)}), s8[4194304]{0:T(1024)(128)(4,1)S(1)}, s32[]{:S(2)}) async-start(s8[8388608]{0:T(1024)(128)(4,1)} %bitcast.340), calls=%async_computation.7 | async-start | bytes 8388608
  412.7 4.2 copy-start.12
  426.4 8.1 %copy-start.11 = (bf16[1,4096,128]{2,1,0:T(8,128)(2,1)S(1)}, bf16[1,4096,128]{2,1,0:T(8,128)(2,1)}, u32[]{:S(2)}) copy-start(bf16[1,4096,128]{2,1,0:T(8,128)(2,1)} %param.29) | copy-start | bytes 3145732
  451.0 3.6 slice-start.2
  451.9 2.9 slice-start.3
  494.0 141.8 %copy-start.2 = (bf16[1,128,4096]{2,1,0:T(8,128)(2,1)S(1)}, bf16[1,128,4096]{2,1,0:T(8,128)(2,1)}, u32[]{:S(2)}) copy-start(bf16[1,128,4096]{2,1,0:T(8,128)(2,1)} %param.22) | copy-start | bytes 3145732
  494.0 141.8 %copy-start.19 = (f32[1,4096]{1,0:T(1,128)S(1)}, f32[1,4096]{1,0:T(1,128)}, u32[]{:S(2)}) copy-start(f32[1,4096]{1,0:T(1,128)} %param.26) | copy-start | bytes 49156
  494.3 143.2 %copy-start.5 = (bf16[1,128,4096]{2,1,0:T(8,128)(2,1)S(1)}, bf16[1,128,4096]{2,1,0:T(8,128)(2,1)}, u32[]{:S(2)}) copy-start(bf16[1,128,4096]{2,1,0:T(8,128)(2,1)} %param.23) | copy-start | bytes 3145732
  494.3 143.2 %copy-start.21 = (f32[128]{0:T(128)S(1)}, f32[128]{0:T(128)}, u32[]{:S(2)}) copy-start(f32[128]{0:T(128)} %copy-done.20) | copy-start | bytes 1540
  494.3 143.2 %copy-start.22 = (f32[128]{0:T(128)S(1)}, f32[128]{0:T(128)}, u32[]{:S(2)}) copy-start(f32[128]{0:T(128)} %get-tuple-element.102) | copy-start | bytes 1540
  496.1 146.0 %collective-permute-start = (bf16[128,4096]{1,0:T(8,128)(2,1)}, bf16[128,4096]{1,0:T(8,128)(2,1)}, u32[]{:S(2)}, u32[]{:S(2)}) collective-permute-start(bf16[128,4096]{1,0:T(8,128)(2,1)} %fusion.32), channel_id=1, source_target_pairs={{0,8},{8,16},{16,24},{24,32},{32,40},{40,48},{48,56},{56,64},{64,7... | collective-permute-start | bytes 3145736 | tf_op jit(solution)/shard_map/ppermute | solution.py:17
  639.6 19.7 %collective-permute-start.1 = (bf16[128,4096]{1,0:T(8,128)(2,1)S(1)}, bf16[128,4096]{1,0:T(8,128)(2,1)S(1)}, u32[]{:S(2)}, u32[]{:S(2)}) collective-permute-start(bf16[128,4096]{1,0:T(8,128)(2,1)S(1)} %fusion.40), channel_id=1, source_target_pairs={{8,0},{16,8},{24,16},{32,24},{40,32},{48,40},{56,48},{64,56},{72,6... | collective-permute-start | bytes 3145736 | tf_op jit(solution)/shard_map/ppermute | solution.py:17
  (11 other events, 18.0 us)
Sparse Core Ops, SparseCore 0:
  15.2 179.6 all-gather.4
  197.1 174.1 all-gather.2
  449.9 185.8 reduce-scatter.1
where the time goes:
time: 681 us; the launch traced here: 669 us
  waiting for transfers between devices  471 us (69%)
  matrix products  84.4 us (12%)
  other arithmetic  34.4 us (5%)
  blocking collectives  29.1 us (4%)
  local copies, waits for them, and re-layouts  23.2 us (3%)
  between operations  14.5 us (2%)
  starting transfers between devices  13.2 us (2%)
    all_gather x1, waiting for transfers between devices, body(): forward_whole = lax.all_gather(forward_normed, 'seq', axis=0, tiled=True)  163 us
    all_gather x1, waiting for transfers between devices, body(): back_whole = lax.all_gather(back_normed, 'seq', axis=0, tiled=True)  148 us
    reduce_scatter x1, waiting for transfers between devices, body(): lax.psum_scatter((term + jnp.einsum('tc,rc->tr', value_grad, weights[2],...  135 us
    all_to_all x1, blocking collectives, body(): lax.all_to_all(mixed_rows, 'seq', split_axis=0, concat_axis=1, tiled=True)  29.1 us
    ppermute x2, waiting for transfers between devices, passed_along(): return lax.ppermute(shard, axis, pairs)  17.2 us
    dot_general x1, matrix products, body(): jnp.einsum('tc,rc->tr', value_grad, weights[2], preferred_element_type=jn...  15.3 us
    dot_general x2, matrix products, heads_inputs(): jnp.dot(rows_whole, query_weight, preferred_element_type=jnp.float32)  14.3 us
  transfers between devices with their start and end apart: 6, of which 5 were waited for; matrix products, arithmetic and copies ran while one was open for 8% of the time, Pallas kernels for 0%

commit v1 on v0

--- a/solution.py
+++ b/solution.py
@@ -1,7 +1,17 @@
+import functools
+
 import jax
 import jax.numpy as jnp
 from jax import lax
+from jax.experimental import pallas as pl
+from jax.experimental.pallas import tpu as pltpu
 from jax.sharding import PartitionSpec as P
+
+MESH = pl.DeviceIdType.MESH
+ROWS = 128
+COLS = 4096
+HEADS_WIDE = 512
+ALL_WIDE = 768
 
 MODEL_WIDTH = 4096
 HEAD_SIZE = 128
@@ -146,25 +156,451 @@
     return lax.rsqrt(jnp.mean(hidden * hidden, axis=-1, keepdims=True) + epsilon)
 
 
-def heads_inputs(rows_whole, weights):
-    query_weight, key_matrix, value_matrix = weights
-    sequence_length = rows_whole.shape[0]
-    cosines, sines = rotation_tables(jnp.arange(sequence_length, dtype=jnp.float32))
-    query_proj = jnp.dot(rows_whole, query_weight, preferred_element_type=jnp.float32)
-    key_projected_rows = jnp.dot(rows_whole, key_matrix, preferred_element_type=jnp.float32)
-    value_projected_rows = jnp.dot(rows_whole, value_matrix, preferred_element_type=jnp.float32)
-    query_rows_local = (
-        rotate(query_proj.reshape(sequence_length, -1, HEAD_SIZE), cosines, sines, 1.0)
-        .reshape(sequence_length, -1)
-        .astype(jnp.bfloat16)
-    )
-    key_rows = (
-        rotate(key_projected_rows.reshape(sequence_length, -1, HEAD_SIZE), cosines, sines, 1.0)
-        .reshape(sequence_length, -1)
-        .astype(jnp.bfloat16)
-    )
-    value_rows = value_projected_rows.astype(jnp.bfloat16)
-    return (query_rows_local, key_rows, value_rows, cosines, sines)
+def place():
+    me = lax.axis_index("seq")
+    return me, me // 2, me % 2
+
+
+def peer_of(x, z):
+    return 2 * (x % 4) + z
+
+
+class Copies:
+    def __init__(self, send_sems, recv_sems):
+        self.send_sems, self.recv_sems = send_sems, recv_sems
+        self.sent = []
+
+    def copy(self, number, src, dst, peer):
+        return pltpu.make_async_remote_copy(
+            src_ref=src,
+            dst_ref=dst,
+            send_sem=self.send_sems.at[number],
+            recv_sem=self.recv_sems.at[number],
+            device_id={"seq": peer},
+            device_id_type=MESH,
+        )
+
+    def send(self, number, src, dst, peer):
+        one = self.copy(number, src, dst, peer)
+        one.start()
+        self.sent.append(one)
+
+    def arrived(self, number, dst, peer):
+        self.copy(number, dst, dst, peer).wait_recv()
+
+    def finish(self):
+        for one in self.sent:
+            one.wait_send()
+
+
+def greet(peers):
+    barrier = pltpu.get_barrier_semaphore()
+    for peer in peers:
+        pl.semaphore_signal(barrier, inc=1, device_id={"seq": peer}, device_id_type=MESH)
+    pl.semaphore_wait(barrier, len(peers))
+
+
+def load_weights(weight_refs, whole_weight, sems):
+    query_ref, key_ref, value_ref = weight_refs
+    copies = [
+        pltpu.make_async_copy(query_ref, whole_weight.at[:, 0:512], sems.at[0]),
+        pltpu.make_async_copy(key_ref, whole_weight.at[:, 512:640], sems.at[1]),
+        pltpu.make_async_copy(value_ref, whole_weight.at[:, 640:768], sems.at[2]),
+    ]
+    for one in copies:
+        one.start()
+    return copies
+
+
+def project_rows(pair, whole, weight, cos_ref, sin_ref, out_ref):
+    begin = pl.multiple_of(pair * 256, 256)
+    rows = pl.ds(begin, 256)
+
+    @pl.loop(0, 3)
+    def _(chunk):
+        cols = pl.multiple_of(chunk * 256, 256)
+        product = jnp.dot(
+            whole[rows, :], weight[:, pl.ds(cols, 256)], preferred_element_type=jnp.float32
+        )
+        cosines, sines = cos_ref[rows, :], sin_ref[rows, :]
+        first, second = product[:, :128], product[:, 128:]
+        first_turned = first * cosines + pltpu.roll(first, 64, 1) * sines
+        second_turned = second * cosines + pltpu.roll(second, 64, 1) * sines
+        second_turned = jnp.where(chunk == 2, second, second_turned)
+        out_ref[rows, pl.ds(cols, 128)] = first_turned.astype(jnp.bfloat16)
+        out_ref[rows, pl.ds(pl.multiple_of(cols + 128, 128), 128)] = second_turned.astype(
+            jnp.bfloat16
+        )
+
+
+def gather_plan(copies, own, whole):
+    me, x, z = place()
+    right, left, partner = peer_of(x + 1, z), peer_of(x + 3, z), peer_of(x, 1 - z)
+
+    def part(xx, zz, offset, count):
+        start = pl.multiple_of(peer_of(xx, zz) * ROWS + offset, 32)
+        return whole.at[pl.ds(start, count), :]
+
+    def own_part(offset, count):
+        return own.at[pl.ds(offset, count), :]
+
+    def send(number, peer, xx, zz, offset, count):
+        copies.send(number, part(xx, zz, offset, count), part(xx, zz, offset, count), peer)
+
+    def got(number, peer, xx, zz, offset, count):
+        copies.arrived(number, part(xx, zz, offset, count), peer)
+
+    def begin():
+        low, high = own_part(0, 64), own_part(64, 64)
+        copies.send(0, low, part(x, z, 0, 64), partner)
+        copies.send(6, high, part(x, z, 64, 64), right)
+        copies.send(12, high, part(x, z, 64, 64), left)
+        copies.send(7, low, part(x, z, 0, 64), right)
+        copies.send(13, low, part(x, z, 0, 64), left)
+        copies.send(1, high, part(x, z, 64, 64), partner)
+
+    def relay_partner():
+        got(0, partner, x, 1 - z, 0, 64)
+        send(8, right, x, 1 - z, 0, 64)
+        send(14, left, x, 1 - z, 0, 64)
+
+    def relay_high():
+        got(6, left, x + 3, z, 64, 64)
+        send(9, right, x + 3, z, 64, 32)
+        send(2, partner, x + 3, z, 64, 64)
+        got(12, right, x + 1, z, 64, 64)
+        send(15, left, x + 1, z, 96, 32)
+        send(3, partner, x + 1, z, 64, 64)
+
+    def relay_low():
+        got(7, left, x + 3, z, 0, 64)
+        send(10, right, x + 3, z, 0, 32)
+        got(13, right, x + 1, z, 0, 64)
+        send(16, left, x + 1, z, 32, 32)
+
+    def own_pair():
+        got(1, partner, x, 1 - z, 64, 64)
+
+    def relay_far():
+        got(9, left, x + 2, z, 64, 32)
+        send(4, partner, x + 2, z, 64, 32)
+        got(15, right, x + 2, z, 96, 32)
+        send(5, partner, x + 2, z, 96, 32)
+
+    def relay_partner_low():
+        got(8, left, x + 3, 1 - z, 0, 64)
+        send(11, right, x + 3, 1 - z, 0, 32)
+        got(14, right, x + 1, 1 - z, 0, 64)
+        send(17, left, x + 1, 1 - z, 32, 32)
+
+    def left_pair():
+        got(2, partner, x + 3, 1 - z, 64, 64)
+
+    def right_pair():
+        got(3, partner, x + 1, 1 - z, 64, 64)
+
+    def far_pair():
+        got(10, left, x + 2, z, 0, 32)
+        got(16, right, x + 2, z, 32, 32)
+        got(11, left, x + 2, 1 - z, 0, 32)
+        got(17, right, x + 2, 1 - z, 32, 32)
+        got(4, partner, x + 2, 1 - z, 64, 32)
+        got(5, partner, x + 2, 1 - z, 96, 32)
+
+    return (
+        begin,
+        relay_partner,
+        relay_high,
+        relay_low,
+        own_pair,
+        relay_far,
+        relay_partner_low,
+        left_pair,
+        right_pair,
+        far_pair,
+    )
+
+
+GATHER_COPIES = 18
+
+
+def gather_kernel(exchange, *refs):
+    if exchange:
+        (own, query_ref, key_ref, value_ref, cos_ref, sin_ref, grad_ref, out_ref, heads_ref) = refs[:9]
+        refs = refs[9:]
+    else:
+        (own, query_ref, key_ref, value_ref, cos_ref, sin_ref, out_ref) = refs[:7]
+        refs = refs[7:]
+    whole, weight, local_sems, send_sems, recv_sems = refs
+    me, x, z = place()
+    loads = load_weights((query_ref, key_ref, value_ref), weight, local_sems)
+    mine = pltpu.make_async_copy(
+        own, whole.at[pl.ds(pl.multiple_of(me * ROWS, ROWS), ROWS), :], local_sems.at[3]
+    )
+    mine.start()
+    if exchange:
+        peers = [(me + step) % 8 for step in range(1, 8)]
+    else:
+        peers = [peer_of(x + 1, z), peer_of(x + 3, z), peer_of(x, 1 - z)]
+    greet(peers)
+    copies = Copies(send_sems, recv_sems)
+    (
+        begin,
+        relay_partner,
+        relay_high,
+        relay_low,
+        own_pair,
+        relay_far,
+        relay_partner_low,
+        left_pair,
+        right_pair,
+        far_pair,
+    ) = gather_plan(copies, own, whole)
+    begin()
+
+    def heads_rows(peer):
+        return heads_ref.at[pl.ds(pl.multiple_of(peer * ROWS, ROWS), ROWS), :]
+
+    def grad_cols(peer):
+        return grad_ref.at[:, pl.ds(pl.multiple_of(peer * HEADS_WIDE, HEADS_WIDE), HEADS_WIDE)]
+
+    if exchange:
+        kept = pltpu.make_async_copy(grad_cols(me), heads_rows(me), local_sems.at[4])
+        kept.start()
+    relay_partner()
+    relay_high()
+    relay_low()
+    if exchange:
+        for step in range(1, 8):
+            peer = (me + step) % 8
+            copies.send(GATHER_COPIES + step - 1, grad_cols(peer), heads_rows(me), peer)
+    for one in loads:
+        one.wait()
+    mine.wait()
+    own_pair()
+    project_rows(x, whole, weight, cos_ref, sin_ref, out_ref)
+    relay_partner_low()
+    relay_far()
+    left_pair()
+    project_rows((x + 3) % 4, whole, weight, cos_ref, sin_ref, out_ref)
+    right_pair()
+    project_rows((x + 1) % 4, whole, weight, cos_ref, sin_ref, out_ref)
+    far_pair()
+    project_rows((x + 2) % 4, whole, weight, cos_ref, sin_ref, out_ref)
+    if exchange:
+        kept.wait()
+        for step in range(1, 8):
+            peer = (me + 8 - step) % 8
+            copies.arrived(GATHER_COPIES + step - 1, heads_rows(peer), peer)
+    copies.finish()
+
+
+def gather_project(own, weights, cosines, sines, collective_id, grad=None):
+    exchange = grad is not None
+    vmem = pl.BlockSpec(memory_space=pltpu.VMEM)
+    anywhere = pl.BlockSpec(memory_space=pl.ANY)
+    count = GATHER_COPIES + (7 if exchange else 0)
+    out_shape = [jax.ShapeDtypeStruct((1024, ALL_WIDE), jnp.bfloat16)]
+    operands = [own, *weights, cosines, sines]
+    in_specs = [vmem, anywhere, anywhere, anywhere, vmem, vmem]
+    if exchange:
+        out_shape.append(jax.ShapeDtypeStruct((1024, HEADS_WIDE), jnp.bfloat16))
+        operands.append(grad)
+        in_specs.append(vmem)
+    return pl.pallas_call(
+        functools.partial(gather_kernel, exchange),
+        out_shape=out_shape,
+        in_specs=in_specs,
+        out_specs=[vmem] * len(out_shape),
+        scratch_shapes=[
+            pltpu.VMEM((1024, COLS), jnp.bfloat16),
+            pltpu.VMEM((COLS, ALL_WIDE), jnp.bfloat16),
+            pltpu.SemaphoreType.DMA((5,)),
+            pltpu.SemaphoreType.DMA((count,)),
+            pltpu.SemaphoreType.DMA((count,)),
+        ],
+        compiler_params=pltpu.CompilerParams(
+            collective_id=collective_id, has_side_effects=True
+        ),
+    )(*operands)
+
+
+def add_rows(out, terms, count, chunk=256):
+    @pl.loop(0, count // chunk)
+    def _(step):
+        rows = pl.ds(pl.multiple_of(step * chunk, chunk), chunk)
+        total = terms[0][rows, :].astype(jnp.float32)
+        for term in terms[1:]:
+            total = total + term[rows, :].astype(jnp.float32)
+        out[rows, :] = total.astype(jnp.bfloat16)
+
+
+def reduce_kernel(
+    turned,
+    query_ref,
+    key_ref,
+    value_ref,
+    mixed_ref,
+    sum_ref,
+    owned_ref,
+    weight,
+    shares,
+    z_in,
+    far_right,
+    far_left,
+    near_right,
+    near_left,
+    far_right_one,
+    far_left_one,
+    near_right_one,
+    near_left_one,
+    z_last,
+    local_sems,
+    send_sems,
+    recv_sems,
+):
+    me, x, z = place()
+    loads = load_weights((query_ref, key_ref, value_ref), weight, local_sems)
+    greet([(me + step) % 8 for step in range(1, 8)])
+    copies = Copies(send_sems, recv_sems)
+    right, left, partner = peer_of(x + 1, z), peer_of(x + 3, z), peer_of(x, 1 - z)
+
+    def owned_cols(peer):
+        return owned_ref.at[:, pl.ds(pl.multiple_of(peer * HEADS_WIDE, HEADS_WIDE), HEADS_WIDE)]
+
+    def mixed_rows(peer):
+        return mixed_ref.at[pl.ds(pl.multiple_of(peer * ROWS, ROWS), ROWS), :]
+
+    kept = pltpu.make_async_copy(mixed_rows(me), owned_cols(me), local_sems.at[3])
+    kept.start()
+    for one in loads:
+        one.wait()
+
+    def share(xx, zz, offset, count):
+        return shares.at[peer_of(xx, zz), pl.ds(offset, count), :]
+
+    def pair_share(xx, offset, count):
+        return shares.at[pl.ds(2 * (xx % 4), 2), pl.ds(offset, count), :]
+
+    def compute(delta):
+        pair = (x + delta) % 4
+
+        @pl.loop(0, 8)
+        def _(step):
+            rows = pl.ds(pl.multiple_of(step * 512, 512), 512)
+            product = jnp.dot(weight[rows, :], turned[pair], preferred_element_type=jnp.float32)
+            shares[2 * pair, rows, :] = product[:, :128].astype(jnp.bfloat16)
+            shares[2 * pair + 1, rows, :] = product[:, 128:].astype(jnp.bfloat16)
+
+        copies.send(delta, share(x + delta, 1 - z, 0, 2048), z_in.at[delta], partner)
+
+    compute(2)
+    copies.send(5, pair_share(x + 2, 2048, 1024), far_right, right)
+    copies.send(11, pair_share(x + 2, 3072, 1024), far_left, left)
+    compute(1)
+    copies.send(6, pair_share(x + 1, 3072, 1024), near_right.at[:, pl.ds(1024, 1024), :], right)
+    compute(3)
+    copies.send(12, pair_share(x + 3, 2048, 1024), near_left.at[:, pl.ds(0, 1024), :], left)
+    compute(0)
+    copies.arrived(5, far_right, left)
+    for zz in range(2):
+        spot = shares.at[2 * ((x + 1) % 4) + zz, pl.ds(2048, 1024), :]
+        add_rows(spot, [spot, far_right.at[zz]], 1024)
+    copies.send(7, pair_share(x + 1, 2048, 1024), near_right.at[:, pl.ds(0, 1024), :], right)
+    copies.arrived(11, far_left, right)
+    for zz in range(2):
+        spot = shares.at[2 * ((x + 3) % 4) + zz, pl.ds(3072, 1024), :]
+        add_rows(spot, [spot, far_left.at[zz]], 1024)
+    copies.send(13, pair_share(x + 3, 3072, 1024), near_left.at[:, pl.ds(1024, 1024), :], left)
+    copies.arrived(2, z_in.at[2], partner)
+    spot = share(x + 2, z, 0, 2048)
+    add_rows(spot, [spot, z_in.at[2]], 2048)
+    copies.send(8, share(x + 2, z, 0, 1024), far_right_one, right)
+    copies.send(14, share(x + 2, z, 1024, 1024), far_left_one, left)
+    for step in range(1, 8):
+        peer = (me + step) % 8
+        copies.send(16 + step, mixed_rows(peer), owned_cols(me), peer)
+    copies.arrived(1, z_in.at[1], partner)
+    spot = share(x + 1, z, 1024, 1024)
+    add_rows(spot, [spot, z_in.at[1, pl.ds(1024, 1024), :]], 1024)
+    copies.send(9, spot, near_right_one.at[pl.ds(1024, 1024), :], right)
+    copies.arrived(3, z_in.at[3], partner)
+    spot = share(x + 3, z, 0, 1024)
+    add_rows(spot, [spot, z_in.at[3, pl.ds(0, 1024), :]], 1024)
+    copies.send(15, spot, near_left_one.at[pl.ds(0, 1024), :], left)
+    copies.arrived(8, far_right_one, left)
+    spot = share(x + 1, z, 0, 1024)
+    add_rows(spot, [spot, z_in.at[1, pl.ds(0, 1024), :], far_right_one], 1024)
+    copies.send(10, spot, near_right_one.at[pl.ds(0, 1024), :], right)
+    copies.arrived(14, far_left_one, right)
+    spot = share(x + 3, z, 1024, 1024)
+    add_rows(spot, [spot, z_in.at[3, pl.ds(1024, 1024), :], far_left_one], 1024)
+    copies.send(16, spot, near_left_one.at[pl.ds(1024, 1024), :], left)
+    copies.arrived(6, near_right.at[:, pl.ds(1024, 1024), :], left)
+    copies.arrived(12, near_left.at[:, pl.ds(0, 1024), :], right)
+    copies.arrived(7, near_right.at[:, pl.ds(0, 1024), :], left)
+    copies.arrived(13, near_left.at[:, pl.ds(1024, 1024), :], right)
+    spot = share(x, 1 - z, 2048, 2048)
+    add_rows(spot, [spot, near_right.at[1 - z], near_left.at[1 - z]], 2048)
+    copies.send(4, spot, z_last, partner)
+
+    def total(terms, offset):
+        @pl.loop(0, 8)
+        def _(step):
+            rows = pl.ds(pl.multiple_of(step * 256, 256), 256)
+            summed = terms[0][rows, :].astype(jnp.float32)
+            for term in terms[1:]:
+                summed = summed + term[rows, :].astype(jnp.float32)
+            sum_ref[:, pl.ds(pl.multiple_of(offset + step * 256, 256), 256)] = summed.T
+
+    copies.arrived(0, z_in.at[0], partner)
+    copies.arrived(9, near_right_one.at[pl.ds(1024, 1024), :], left)
+    copies.arrived(15, near_left_one.at[pl.ds(0, 1024), :], right)
+    copies.arrived(10, near_right_one.at[pl.ds(0, 1024), :], left)
+    copies.arrived(16, near_left_one.at[pl.ds(1024, 1024), :], right)
+    total([share(x, z, 0, 2048), z_in.at[0], near_right_one, near_left_one], 0)
+    kept.wait()
+    for step in range(1, 8):
+        peer = (me + 8 - step) % 8
+        copies.arrived(16 + step, owned_cols(peer), peer)
+    copies.arrived(4, z_last, partner)
+    total([share(x, z, 2048, 2048), near_right.at[z], near_left.at[z], z_last], 2048)
+    copies.finish()
+
+
+def reduce_project(turned, weights, mixed, collective_id):
+    vmem = pl.BlockSpec(memory_space=pltpu.VMEM)
+    anywhere = pl.BlockSpec(memory_space=pl.ANY)
+    bf16 = jnp.bfloat16
+    return pl.pallas_call(
+        reduce_kernel,
+        out_shape=[
+            jax.ShapeDtypeStruct((ROWS, COLS), jnp.float32),
+            jax.ShapeDtypeStruct((ROWS, COLS), bf16),
+        ],
+        in_specs=[vmem, anywhere, anywhere, anywhere, vmem],
+        out_specs=[vmem, vmem],
+        scratch_shapes=[
+            pltpu.VMEM((COLS, ALL_WIDE), bf16),
+            pltpu.VMEM((8, COLS, ROWS), bf16),
+            pltpu.VMEM((4, 2048, ROWS), bf16),
+            pltpu.VMEM((2, 1024, ROWS), bf16),
+            pltpu.VMEM((2, 1024, ROWS), bf16),
+            pltpu.VMEM((2, 2048, ROWS), bf16),
+            pltpu.VMEM((2, 2048, ROWS), bf16),
+            pltpu.VMEM((1024, ROWS), bf16),
+            pltpu.VMEM((1024, ROWS), bf16),
+            pltpu.VMEM((2048, ROWS), bf16),
+            pltpu.VMEM((2048, ROWS), bf16),
+            pltpu.VMEM((2048, ROWS), bf16),
+            pltpu.SemaphoreType.DMA((4,)),
+            pltpu.SemaphoreType.DMA((24,)),
+            pltpu.SemaphoreType.DMA((24,)),
+        ],
+        compiler_params=pltpu.CompilerParams(
+            collective_id=collective_id, has_side_effects=True
+        ),
+    )(turned, *weights, mixed)
 
 
 def body(
@@ -188,29 +624,33 @@
     back_hidden = saved_rows[0].astype(jnp.float32)
     back_scale = token_scale(back_hidden)
     back_normed = (back_hidden * back_scale * gain_row).astype(jnp.bfloat16)
-    forward_whole = lax.all_gather(forward_normed, "seq", axis=0, tiled=True)
-    query_rows_local, key_rows, value_rows, cosines, sines = heads_inputs(forward_whole, weights)
-    mixed_rows = attend(query_rows_local, key_rows, value_rows, first_docs)
-    mixed_rows = lax.all_to_all(mixed_rows, "seq", split_axis=0, concat_axis=1, tiled=True)
-    first_out = (forward_hidden + mixed_rows.astype(jnp.float32)).astype(jnp.bfloat16)
+    cosines, sines = rotation_tables(jnp.arange(8 * ROWS, dtype=jnp.float32))
+    cos_wide = jnp.concatenate([cosines, cosines], 1)
+    sin_wide = jnp.concatenate([-sines, sines], 1)
+    (forward_heads,) = gather_project(forward_normed, weights, cos_wide, sin_wide, 0)
+    mixed_rows = attend(
+        forward_heads[:, :512], forward_heads[:, 512:640], forward_heads[:, 640:], first_docs
+    )
+    back_heads, head_gradients = gather_project(
+        back_normed, weights, cos_wide, sin_wide, 1, output_grad[0]
+    )
+    query_grad, key_grad, value_grad = attend_back(
+        back_heads[:, :512],
+        back_heads[:, 512:640],
+        back_heads[:, 640:],
+        head_gradients,
+        back_docs,
+        cosines,
+        sines,
+    )
+    turned = (
+        jnp.concatenate([query_grad, key_grad, value_grad], 1)
+        .reshape(4, 256, ALL_WIDE)
+        .transpose(0, 2, 1)
+    )
+    input_sum, owned_rows = reduce_project(turned, weights, mixed_rows, 2)
+    first_out = (forward_hidden + owned_rows.astype(jnp.float32)).astype(jnp.bfloat16)
     section_output = passed_along(first_out, "section", 1)
-    back_whole = lax.all_gather(back_normed, "seq", axis=0, tiled=True)
-    head_gradients = lax.all_to_all(output_grad[0], "seq", split_axis=1, concat_axis=0, tiled=True)
-    query_rows_local, key_rows, value_rows, cosines, sines = heads_inputs(back_whole, weights)
-    query_grad, key_grad, value_grad = attend_back(
-        query_rows_local, key_rows, value_rows, head_gradients, back_docs, cosines, sines
-    )
-    term = jnp.einsum("tc,rc->tr", query_grad, weights[0], preferred_element_type=jnp.float32)
-    term = term + jnp.einsum("tc,rc->tr", key_grad, weights[1], preferred_element_type=jnp.float32)
-    input_sum = lax.psum_scatter(
-        (
-            term
-            + jnp.einsum("tc,rc->tr", value_grad, weights[2], preferred_element_type=jnp.float32)
-        ).astype(jnp.bfloat16),
-        "seq",
-        scatter_dimension=0,
-        tiled=True,
-    ).astype(jnp.float32)
     gained = gain_row * input_sum
     inner_sum = jnp.sum(back_hidden * gained, axis=-1, keepdims=True)
     norm_part = (

time: 681 us -> 347 us (0.51)
  waiting for transfers between devices: 471 us -> 11.7 us
  Pallas kernels: 0 us -> 219 us
  matrix products: 84.4 us -> 36.3 us
  blocking collectives: 29.1 us -> 0 us
  between operations: 14.5 us -> 1.38 us
    all_gather x2 -> x0, waiting for transfers between devices: 311 us -> none  [the longest x1 163 us: body(): forward_whole = lax.all_gather(forward_normed, 'seq', axis=0, tiled=True)]
    pallas_call x0 -> x3, Pallas kernels: none -> 219 us  [the longest x2 142 us: gather_project(): pl.pallas_call(functools.partial(gather_kernel, exchange), out_shape=out_...]
    reduce_scatter x1 -> x0, waiting for transfers between devices: 135 us -> none  [body(): lax.psum_scatter((term + jnp.einsum('tc,rc->tr', value_grad, weights[2],...]
    dot_general x9 -> x0, matrix products: 60.3 us -> none  [the longest x1 15.3 us: body(): jnp.einsum('tc,rc->tr', value_grad, weights[2], preferred_element_type=jn...]
    all_to_all x1 -> x0, blocking collectives: 29.1 us -> none  [body(): lax.all_to_all(mixed_rows, 'seq', split_axis=0, concat_axis=1, tiled=True)]
  transfers between devices with their start and end apart: 6 -> 2, of which waited for: 5 -> 2; matrix products, arithmetic and copies ran while one was open for 8% -> 0% of each run, Pallas kernels for 0% -> 0%
where the time goes in v1:
time: 347 us; the launch traced here: 341 us
  Pallas kernels  219 us (63%)
  matrix products  36.3 us (10%)
  other arithmetic  32.9 us (9%)
  local copies, waits for them, and re-layouts  29.4 us (8%)
  waiting for transfers between devices  11.7 us (3%)
  starting transfers between devices  9.78 us (3%)
    pallas_call x2, Pallas kernels, gather_project(): pl.pallas_call(functools.partial(gather_kernel, exchange), out_shape=out_...  142 us
    pallas_call x1, Pallas kernels, reduce_project(): pl.pallas_call(reduce_kernel, out_shape=[jax.ShapeDtypeStruct((ROWS, COLS...  77.3 us
    ppermute x2, waiting for transfers between devices, passed_along(): return lax.ppermute(shard, axis, pairs)  11.7 us
    ppermute x2, starting transfers between devices, passed_along(): return lax.ppermute(shard, axis, pairs)  9.78 us
    dot_general x4, matrix products, block_probs(): jnp.einsum('tjgd,sjd->jgts', query_block, key_heads, preferred_element_ty...  8.8 us
    dot_general x2, matrix products, attend(): jnp.einsum('jgts,sjd->tjgd', probability, value_heads[:end_row], preferre...  7.32 us
    dot_general x2, matrix products, attend_back(): jnp.einsum('tjgd,sjd->jgts', grad_block, value_heads[:end_row], preferred...  7.1 us
  transfers between devices with their start and end apart: 2, of which 2 were waited for; matrix products, arithmetic and copies ran while one was open for 0% of the time, Pallas kernels for 0%

profile of v1, /device:TPU:25, one launch (start us, length us, event | category | flops | bytes accessed | tf_op | source)
XLA Modules:
  0.0 340.5 jit_solution(10805935422231008606)
XLA Ops:
  14.3 78.8 %shard_map.114 = (bf16[1024,768]{1,0:T(8,128)(2,1)}, bf16[1024,512]{1,0:T(8,128)(2,1)}) custom-call(bf16[128,4096]{1,0:T(8,128)(2,1)} %get-tuple-element.101.refs_0_, bf16[4096,512]{1,0:T(8,128)(2,1)} %bitcast.310, bf16[4096,128]{1,0:T(8,128)(2,1)} %bitcast.313, bf16[4096,128]{1,0:T(8,128)(2,1)} %bitcast.316, f32[1024,128]{1,0:T(8,128)} %get-tuple-element.126.refs_4_, ...), custom_call_target="tpu_custom_call" | custom-call | tf_op jit(solution)/shard_map/pallas_call | solution.py:410
  95.5 2.2 fusion.131
  101.8 2.2 fusion.75
  104.1 2.6 fusion.13
  109.7 2.4 fusion.46
  116.7 63.0 %shard_map.115 = bf16[1024,768]{1,0:T(8,128)(2,1)} custom-call(bf16[128,4096]{1,0:T(8,128)(2,1)} %get-tuple-element.100.refs_0_, bf16[4096,512]{1,0:T(8,128)(2,1)} %bitcast.311, bf16[4096,128]{1,0:T(8,128)(2,1)} %bitcast.314, bf16[4096,128]{1,0:T(8,128)(2,1)} %bitcast.317, f32[1024,128]{1,0:T(8,128)} %get-tuple-element.126.refs_4_, ...), custom_call_target="tpu_custom_call" | custom-call | tf_op jit(solution)/shard_map/pallas_call | solution.py:410
  181.9 2.1 slice_bitcast_fusion.1
  186.9 3.4 fusion.60
  192.6 2.7 fusion.4
  195.3 2.1 fusion.7
  197.4 3.9 %fusion.54 = bf16[512,1,4,128]{0,3,2,1:T(8,128)(2,1)S(1)} fusion(f32[4,512]{1,0:T(4,128)S(1)} %fusion.7, f32[4,512]{1,0:T(4,128)S(1)} %get-tuple-element.117, f32[1024,512,4]{1,0,2:T(8,128)S(1)} %get-tuple-element.118, pred[512,1024]{0,1:T(8,128)(4,1)S(1)} %get-tuple-element.102, bf16[1024,768]{1,0:T(8,128)(2,1)} %shard_map.115), kind=kOutput, calls=%fused_computation.73 | convolution fusion | flops 549715968 | bytes 9715712 | tf_op jit(solution)/shard_map/jgts,sjd->tjgd/dot_general | solution.py:82
  202.5 2.5 copy.120.mixed_ref
  204.9 2.5 fusion.3
  207.5 2.1 fusion.6
  209.6 4.5 %fusion = (f32[4,512]{1,0:T(4,128)S(1)}, f32[1024,512,4]{1,0,2:T(8,128)S(1)}) fusion(f32[4,512]{1,0:T(4,128)S(1)} %fusion.6, f32[4,512]{1,0:T(4,128)S(1)} %get-tuple-element.109, f32[1024,512,4]{1,0,2:T(8,128)S(1)} %get-tuple-element.110, pred[512,1024]{0,1:T(8,128)(4,1)S(1)} %get-tuple-element.103, bf16[512,4,128]{0,2,1:T(8,128)(2,1)S(1)} %bitcast.331, ...), kind=kOutput, calls=%fused_computation.4 | convolution fusion | flops 551548928 | bytes 18112512 | tf_op jit(solution)/shard_map/tjgd,sjd->jgts/dot_general | solution.py:111
  214.1 3.7 %fusion.72 = bf16[1024,128]{0,1:T(8,128)(2,1)} fusion(bf16[512,4,128]{0,2,1:T(8,128)(2,1)S(1)} %bitcast.332, f32[4,512]{1,0:T(4,128)S(1)} %fusion.6, f32[4,512]{1,0:T(4,128)S(1)} %get-tuple-element.109, f32[1024,512,4]{1,0,2:T(8,128)S(1)} %get-tuple-element.110, pred[512,1024]{0,1:T(8,128)(4,1)S(1)} %get-tuple-element.103, f32[512,1,128]{0,2,1:T(8,128)S(1)} %copy-done.26), kind=kOutput, calls=%fused_computation.82 | convolution fusion | flops 549715968 | bytes 9977856 | tf_op jit(solution)/shard_map/jgts,tjgd->sjd/dot_general | solution.py:136
  217.8 2.9 fusion.8
  231.3 2.2 pad_maximum_fusion
  233.6 2.6 copy.96
  236.2 77.3 %shard_map.116 = (f32[128,4096]{1,0:T(8,128)}, bf16[128,4096]{1,0:T(8,128)(2,1)}) custom-call(bf16[4,768,256]{2,1,0:T(8,128)(2,1)} %bitcast.320, bf16[4096,512]{1,0:T(8,128)(2,1)} %bitcast.312, bf16[4096,128]{1,0:T(8,128)(2,1)} %bitcast.315, bf16[4096,128]{1,0:T(8,128)(2,1)} %bitcast.318, bf16[1024,512]{1,0:T(8,128)(2,1)} %copy.120.mixed_ref), custom_call_target="tpu_custom_call" | custom-call | tf_op jit(solution)/shard_map/pallas_call | solution.py:575
  313.5 2.1 fusion.35
  316.6 5.0 %collective-permute-start.1 = (bf16[128,4096]{1,0:T(8,128)(2,1)S(1)}, bf16[128,4096]{1,0:T(8,128)(2,1)S(1)}, u32[]{:S(2)}, u32[]{:S(2)}) collective-permute-start(bf16[128,4096]{1,0:T(8,128)(2,1)S(1)} %fusion.34), channel_id=1, source_target_pairs={{8,0},{16,8},{24,16},{32,24},{40,32},{48,40},{56,48},{64,56},{72,6... | collective-permute-start | bytes 3145736 | tf_op jit(solution)/shard_map/ppermute | solution.py:27
  321.9 4.8 %collective-permute-start = (bf16[128,4096]{1,0:T(8,128)(2,1)S(1)}, bf16[128,4096]{1,0:T(8,128)(2,1)S(1)}, u32[]{:S(2)}, u32[]{:S(2)}) collective-permute-start(bf16[128,4096]{1,0:T(8,128)(2,1)S(1)} %fusion.26), channel_id=1, source_target_pairs={{0,8},{8,16},{16,24},{24,32},{32,40},{40,48},{48,56},{56,64},{64,7... | collective-permute-start | bytes 3145736 | tf_op jit(solution)/shard_map/ppermute | solution.py:27
  326.6 10.3 %collective-permute-done.1 = bf16[128,4096]{1,0:T(8,128)(2,1)S(1)} collective-permute-done((bf16[128,4096]{1,0:T(8,128)(2,1)S(1)}, bf16[128,4096]{1,0:T(8,128)(2,1)S(1)}, u32[]{:S(2)}, u32[]{:S(2)}) %collective-permute-start.1) | collective-permute-done | bytes 1048608 | tf_op jit(solution)/shard_map/ppermute | solution.py:27
  (102 shorter events, 51.3 us)
Async XLA Ops:
  0.6 9.9 %copy-start.24 = (f32[64]{0:T(128)}, f32[64]{0:T(128)S(1)}, u32[]{:S(2)}) copy-start(f32[64]{0:T(128)S(1)} %negate_power_fusion) | copy-start | bytes 772
  1.2 11.1 %copy-start = (bf16[1,128,4096]{2,1,0:T(8,128)(2,1)S(1)}, bf16[1,128,4096]{2,1,0:T(8,128)(2,1)}, u32[]{:S(2)}) copy-start(bf16[1,128,4096]{2,1,0:T(8,128)(2,1)} %param.22) | copy-start | bytes 3145732
  1.2 11.1 %copy-start.1 = (bf16[1,128,4096]{2,1,0:T(8,128)(2,1)S(1)}, bf16[1,128,4096]{2,1,0:T(8,128)(2,1)}, u32[]{:S(2)}) copy-start(bf16[1,128,4096]{2,1,0:T(8,128)(2,1)} %param.21) | copy-start | bytes 3145732
  1.2 11.1 %copy-start.15 = (f32[1,4096]{1,0:T(1,128)S(1)}, f32[1,4096]{1,0:T(1,128)}, u32[]{:S(2)}) copy-start(f32[1,4096]{1,0:T(1,128)} %param.26) | copy-start | bytes 49156
  12.3 80.8 %copy-start.21 = (f32[128]{0:T(128)}, f32[128]{0:T(128)S(1)}, u32[]{:S(2)}) copy-start(f32[128]{0:T(128)S(1)} %get-tuple-element.105) | copy-start | bytes 1540
  108.2 7.7 %copy-start.6 = (f32[512,64]{1,0:T(8,128)S(1)}, f32[512,64]{1,0:T(8,128)}, u32[]{:S(2)}) copy-start(f32[512,64]{1,0:T(8,128)} %get-tuple-element.129) | copy-start | bytes 393220
  109.7 5.4 %copy-start.7 = (f32[512,64]{1,0:T(8,128)S(1)}, f32[512,64]{1,0:T(8,128)}, u32[]{:S(2)}) copy-start(f32[512,64]{1,0:T(8,128)} %get-tuple-element.128) | copy-start | bytes 393220
  186.8 3.5 %copy-start.3 = (f32[512,1,4,128]{0,3,2,1:T(8,128)S(1)}, f32[512,1,4,128]{0,3,2,1:T(8,128)}, u32[]{:S(2)}) copy-start(f32[512,1,4,128]{0,3,2,1:T(8,128)} %fusion.46) | copy-start | bytes 3145732
  186.8 3.5 %copy-start.10 = (f32[512,64]{0,1:T(8,128)S(1)}, f32[512,64]{0,1:T(8,128)}, u32[]{:S(2)}) copy-start(f32[512,64]{0,1:T(8,128)} %copy.76) | copy-start | bytes 393220
  186.8 3.5 %copy-start.11 = (f32[512,64]{0,1:T(8,128)S(1)}, f32[512,64]{0,1:T(8,128)}, u32[]{:S(2)}) copy-start(f32[512,64]{0,1:T(8,128)} %copy.74) | copy-start | bytes 393220
  186.8 4.7 %copy-start.16 = (s32[1,1024]{1,0:T(1,128)S(1)}, s32[1,1024]{1,0:T(1,128)}, u32[]{:S(2)}) copy-start(s32[1,1024]{1,0:T(1,128)} %get-tuple-element.123) | copy-start | bytes 12292
  186.8 4.7 %copy-start.17 = (s32[1,1024]{1,0:T(1,128)S(1)}, s32[1,1024]{1,0:T(1,128)}, u32[]{:S(2)}) copy-start(s32[1,1024]{1,0:T(1,128)} %get-tuple-element.124) | copy-start | bytes 12292
  186.8 4.7 %copy-start.18 = (s32[1,512]{1,0:T(1,128)S(1)}, s32[1,512]{1,0:T(1,128)}, u32[]{:S(2)}) copy-start(s32[1,512]{1,0:T(1,128)} %get-tuple-element.97) | copy-start | bytes 6148
  186.8 4.7 %copy-start.19 = (s32[1,512]{1,0:T(1,128)S(1)}, s32[1,512]{1,0:T(1,128)}, u32[]{:S(2)}) copy-start(s32[1,512]{1,0:T(1,128)} %get-tuple-element.121) | copy-start | bytes 6148
  186.8 4.7 %copy-start.20 = (s32[512]{0:T(512)S(1)}, s32[512]{0:T(512)}, u32[]{:S(2)}) copy-start(s32[512]{0:T(512)} %iota_add_fusion) | copy-start | bytes 6148
  197.4 4.0 %copy-start.14 = (bf16[512,1,4,128]{0,3,2,1:T(8,128)(2,1)S(1)}, bf16[512,1,4,128]{0,3,2,1:T(8,128)(2,1)}, u32[]{:S(2)}) copy-start(bf16[512,1,4,128]{0,3,2,1:T(8,128)(2,1)} %fusion.60) | copy-start | bytes 1572868
  209.6 4.5 %copy-start.26 = (f32[512,1,128]{0,2,1:T(8,128)S(1)}, f32[512,1,128]{0,2,1:T(8,128)}, u32[]{:S(2)}) copy-start(f32[512,1,128]{0,2,1:T(8,128)} %fusion.75) | copy-start | bytes 786436
  220.7 3.3 copy-start.25
  236.2 79.4 %copy-start.4 = (bf16[1,128,4096]{2,1,0:T(8,128)(2,1)S(1)}, bf16[1,128,4096]{2,1,0:T(8,128)(2,1)}, u32[]{:S(2)}) copy-start(bf16[1,128,4096]{2,1,0:T(8,128)(2,1)} %param.23) | copy-start | bytes 3145732
  236.2 79.4 %copy-start.22 = (f32[128]{0:T(128)S(1)}, f32[128]{0:T(128)}, u32[]{:S(2)}) copy-start(f32[128]{0:T(128)} %copy-done.21) | copy-start | bytes 1540
  236.2 79.4 %copy-start.23 = (f32[128]{0:T(128)S(1)}, f32[128]{0:T(128)}, u32[]{:S(2)}) copy-start(f32[128]{0:T(128)} %get-tuple-element.104) | copy-start | bytes 1540
  313.5 8.1 %copy-start.5 = (bf16[128,4096]{1,0:T(8,128)(2,1)S(1)}, bf16[128,4096]{1,0:T(8,128)(2,1)}, u32[]{:S(2)}) copy-start(bf16[128,4096]{1,0:T(8,128)(2,1)} %get-tuple-element.78) | copy-start | bytes 3145732
  316.6 20.3 %collective-permute-start.1 = (bf16[128,4096]{1,0:T(8,128)(2,1)S(1)}, bf16[128,4096]{1,0:T(8,128)(2,1)S(1)}, u32[]{:S(2)}, u32[]{:S(2)}) collective-permute-start(bf16[128,4096]{1,0:T(8,128)(2,1)S(1)} %fusion.34), channel_id=1, source_target_pairs={{8,0},{16,8},{24,16},{32,24},{40,32},{48,40},{56,48},{64,56},{72,6... | collective-permute-start | bytes 3145736 | tf_op jit(solution)/shard_map/ppermute | solution.py:27
  321.9 16.5 %collective-permute-start = (bf16[128,4096]{1,0:T(8,128)(2,1)S(1)}, bf16[128,4096]{1,0:T(8,128)(2,1)S(1)}, u32[]{:S(2)}, u32[]{:S(2)}) collective-permute-start(bf16[128,4096]{1,0:T(8,128)(2,1)S(1)} %fusion.26), channel_id=1, source_target_pairs={{0,8},{8,16},{16,24},{24,32},{32,40},{40,48},{48,56},{56,64},{64,7... | collective-permute-start | bytes 3145736 | tf_op jit(solution)/shard_map/ppermute | solution.py:27
  (5 other events, 11.7 us)

commit v2 on v1

--- a/solution.py
+++ b/solution.py
@@ -34,122 +34,89 @@
     return (jnp.cos(angles), jnp.sin(angles))
 
 
-def rotate(values, cosines, sines, sign):
-    half = values.shape[-1] // 2
-    extra = (1,) * (values.ndim - 2)
-    cos_wide = cosines.reshape(cosines.shape[:1] + extra + cosines.shape[1:])
-    sin_wide = sines.reshape(sines.shape[:1] + extra + sines.shape[1:])
-    first = values[..., :half]
-    second = values[..., half:]
-    return jnp.concatenate(
-        [first * cos_wide - sign * second * sin_wide, second * cos_wide + sign * first * sin_wide],
-        axis=-1,
-    )
-
-
-def pair_mask(row_docs, col_docs, row_begin):
-    row_pos = row_begin + lax.iota(jnp.int32, row_docs.shape[0])
-    col_pos = lax.iota(jnp.int32, col_docs.shape[0])
-    return (col_pos[None, :] <= row_pos[:, None]) & (row_docs[:, None] == col_docs[None, :])
-
-
-def block_probs(query_block, key_heads, allowed):
-    scores = jnp.einsum(
-        "tjgd,sjd->jgts", query_block, key_heads, preferred_element_type=jnp.float32
-    ) * HEAD_SIZE ** (-0.5)
-    scores = jnp.where(allowed, scores, -1e30)
-    row_top = jnp.max(scores, axis=-1, keepdims=True)
-    exp_scores = jnp.where(allowed, jnp.exp(scores - row_top), 0.0)
-    return exp_scores / jnp.sum(exp_scores, axis=-1, keepdims=True)
-
-
-def attend(query_rows_local, key_rows, value_rows, documents):
-    sequence_length = query_rows_local.shape[0]
-    groups = key_rows.shape[1] // HEAD_SIZE
-    group_size = query_rows_local.shape[1] // key_rows.shape[1]
-    query_head_count = query_rows_local.reshape(sequence_length, groups, group_size, HEAD_SIZE)
-    key_heads = key_rows.reshape(sequence_length, groups, HEAD_SIZE)
-    value_heads = value_rows.reshape(sequence_length, groups, HEAD_SIZE)
-    block_rows = min(512, sequence_length)
-    pieces = []
-    for block_index in range(sequence_length // block_rows):
-        begin_row = block_index * block_rows
-        end_row = begin_row + block_rows
-        allowed = pair_mask(documents[begin_row:end_row], documents[:end_row], begin_row)
+def window(block):
+    begin = max(0, block * 256 - 512)
+    return begin, (block + 1) * 256 - begin
+
+
+def set_bias(block, docs_col, docs_row, bias):
+    begin, count = window(block)
+    shape = (count, 256)
+    keys = begin + lax.broadcasted_iota(jnp.int32, shape, 0)
+    queries = block * 256 + lax.broadcasted_iota(jnp.int32, shape, 1)
+    same = docs_col[pl.ds(begin, count), :] == docs_row[:, pl.ds(block * 256, 256)]
+    bias[pl.ds(0, count), :] = jnp.where((keys <= queries) & same, 0.0, -1e30)
+
+
+def across(left, right):
+    return lax.dot_general(
+        left, right, (((1,), (1,)), ((), ())), preferred_element_type=jnp.float32
+    )
+
+
+def block_probs(query, key, bias):
+    scores = across(key, query) * HEAD_SIZE ** (-0.5) + bias
+    exp_scores = jnp.exp(scores - jnp.max(scores, axis=0, keepdims=True))
+    return exp_scores * (1.0 / jnp.sum(exp_scores, axis=0, keepdims=True))
+
+
+def head_cols(head):
+    return pl.ds(pl.multiple_of(head * HEAD_SIZE, HEAD_SIZE), HEAD_SIZE)
+
+
+def attend_block(block, heads, docs_col, docs_row, bias, value_turned, mixed):
+    begin, count = window(block)
+    rows = pl.ds(block * 256, 256)
+    set_bias(block, docs_col, docs_row, bias)
+
+    @pl.loop(0, 4)
+    def _(head):
+        cols = head_cols(head)
         probability = block_probs(
-            query_head_count[begin_row:end_row], key_heads[:end_row], allowed
-        ).astype(jnp.bfloat16)
-        mixed_rows = jnp.einsum(
-            "jgts,sjd->tjgd", probability, value_heads[:end_row], preferred_element_type=jnp.float32
+            heads[rows, cols], heads[pl.ds(begin, count), 512:640], bias[pl.ds(0, count), :]
         )
-        pieces.append(mixed_rows.astype(jnp.bfloat16))
-    return lax.optimization_barrier(
-        jnp.concatenate(pieces, 0).reshape(sequence_length, query_rows_local.shape[1])
-    )
-
-
-def attend_back(query_rows_local, key_rows, value_rows, output_gradient, documents, cosines, sines):
-    sequence_length = query_rows_local.shape[0]
-    groups = key_rows.shape[1] // HEAD_SIZE
-    group_size = query_rows_local.shape[1] // key_rows.shape[1]
-    query_head_count = query_rows_local.reshape(sequence_length, groups, group_size, HEAD_SIZE)
-    key_heads = key_rows.reshape(sequence_length, groups, HEAD_SIZE)
-    value_heads = value_rows.reshape(sequence_length, groups, HEAD_SIZE)
-    head_gradients = output_gradient.reshape(sequence_length, groups, group_size, HEAD_SIZE)
-    scale = HEAD_SIZE ** (-0.5)
-    key_grad = jnp.zeros((sequence_length, groups, HEAD_SIZE), jnp.float32)
-    value_grad = jnp.zeros((sequence_length, groups, HEAD_SIZE), jnp.float32)
-    block_rows = min(512, sequence_length)
-    query_pieces = []
-    for block_index in range(sequence_length // block_rows):
-        begin_row = block_index * block_rows
-        end_row = begin_row + block_rows
-        allowed = pair_mask(documents[begin_row:end_row], documents[:end_row], begin_row)
-        query_block = query_head_count[begin_row:end_row]
-        grad_block = head_gradients[begin_row:end_row]
-        probability = block_probs(query_block, key_heads[:end_row], allowed)
-        grad_probs = jnp.einsum(
-            "tjgd,sjd->jgts", grad_block, value_heads[:end_row], preferred_element_type=jnp.float32
+        turned = jnp.dot(
+            value_turned[:, pl.ds(begin, count)],
+            probability.astype(jnp.bfloat16),
+            preferred_element_type=jnp.float32,
         )
-        row_delta = jnp.sum(probability * grad_probs, axis=-1, keepdims=True)
+        mixed[rows, cols] = turned.T.astype(jnp.bfloat16)
+
+
+def attend_back_block(
+    block, heads, grads, docs_col, docs_row, cos_turned, sin_turned, bias, key_turned, key_grad, value_grad, out
+):
+    begin, count = window(block)
+    rows, keys = pl.ds(block * 256, 256), pl.ds(begin, count)
+    set_bias(block, docs_col, docs_row, bias)
+
+    @pl.loop(0, 4)
+    def _(head):
+        cols = head_cols(head)
+        query, grad = heads[rows, cols], grads[rows, cols]
+        probability = block_probs(query, heads[keys, 512:640], bias[pl.ds(0, count), :])
+        grad_probs = across(heads[keys, 640:768], grad)
+        row_delta = jnp.sum(probability * grad_probs, axis=0, keepdims=True)
         grad_scores = (probability * (grad_probs - row_delta)).astype(jnp.bfloat16)
-        query_piece = (
-            jnp.einsum(
-                "jgts,sjd->tjgd",
-                grad_scores,
-                key_heads[:end_row],
-                preferred_element_type=jnp.float32,
-            )
-            * scale
+        value_grad[keys, :] += jnp.dot(
+            probability.astype(jnp.bfloat16), grad, preferred_element_type=jnp.float32
         )
-        query_piece = rotate(
-            query_piece, cosines[begin_row:end_row], sines[begin_row:end_row], -1.0
+        key_grad[keys, :] += jnp.dot(grad_scores, query, preferred_element_type=jnp.float32)
+        turned = (
+            jnp.dot(key_turned[:, keys], grad_scores, preferred_element_type=jnp.float32)
+            * HEAD_SIZE ** (-0.5)
         )
-        query_pieces.append(query_piece.astype(jnp.bfloat16))
-        key_grad = key_grad.at[:end_row].add(
-            jnp.einsum(
-                "jgts,tjgd->sjd", grad_scores, query_block, preferred_element_type=jnp.float32
-            )
-            * scale
-        )
-        value_grad = value_grad.at[:end_row].add(
-            jnp.einsum(
-                "jgts,tjgd->sjd",
-                probability.astype(jnp.bfloat16),
-                grad_block,
-                preferred_element_type=jnp.float32,
-            )
-        )
-    query_grad = jnp.concatenate(query_pieces, 0).reshape(
-        sequence_length, query_rows_local.shape[1]
-    )
-    key_grad = (
-        rotate(key_grad, cosines, sines, -1.0)
-        .astype(jnp.bfloat16)
-        .reshape(sequence_length, groups * HEAD_SIZE)
-    )
-    value_grad = value_grad.astype(jnp.bfloat16).reshape(sequence_length, groups * HEAD_SIZE)
-    return lax.optimization_barrier((query_grad, key_grad, value_grad))
+        swapped = jnp.concatenate([turned[64:], turned[:64]], 0)
+        turned = turned * cos_turned[:, rows] - swapped * sin_turned[:, rows]
+        out[block, cols, :] = turned.astype(jnp.bfloat16)
+
+
+def finish_back(block, cos_ref, sin_ref, key_grad, value_grad, out):
+    rows = pl.ds(block * 256, 256)
+    keys = key_grad[rows, :] * HEAD_SIZE ** (-0.5)
+    keys = keys * cos_ref[rows, :] - pltpu.roll(keys, 64, 1) * sin_ref[rows, :]
+    out[block, 512:640, :] = keys.T.astype(jnp.bfloat16)
+    out[block, 640:768, :] = value_grad[rows, :].T.astype(jnp.bfloat16)
 
 
 def token_scale(hidden):
@@ -325,13 +292,44 @@
 
 
 def gather_kernel(exchange, *refs):
+    own, query_ref, key_ref, value_ref, cos_ref, sin_ref = refs[:6]
+    refs = refs[6:]
     if exchange:
-        (own, query_ref, key_ref, value_ref, cos_ref, sin_ref, grad_ref, out_ref, heads_ref) = refs[:9]
-        refs = refs[9:]
+        grad_ref, out_ref, heads_ref, whole, weight, local_sems, send_sems, recv_sems = refs
+        blocks = [lambda: None] * 4
     else:
-        (own, query_ref, key_ref, value_ref, cos_ref, sin_ref, out_ref) = refs[:7]
-        refs = refs[7:]
-    whole, weight, local_sems, send_sems, recv_sems = refs
+        back_heads, back_grads, docs_col, docs_row, cos_turned, sin_turned = refs[:6]
+        out_ref, back_out, whole, weight, local_sems, send_sems, recv_sems = refs[6:13]
+        bias, key_turned, key_grad, value_grad = refs[13:]
+
+        def back(block):
+            attend_back_block(
+                block,
+                back_heads,
+                back_grads,
+                docs_col,
+                docs_row,
+                cos_turned,
+                sin_turned,
+                bias,
+                key_turned,
+                key_grad,
+                value_grad,
+                back_out,
+            )
+
+        def first_block():
+            key_turned[...] = back_heads[:, 512:640].astype(jnp.float32).T.astype(jnp.bfloat16)
+            key_grad[...] = jnp.zeros_like(key_grad)
+            value_grad[...] = jnp.zeros_like(value_grad)
+            back(0)
+
+        def last_block():
+            back(3)
+            for block in range(4):
+                finish_back(block, cos_ref, sin_ref, key_grad, value_grad, back_out)
+
+        blocks = [first_block, lambda: back(1), lambda: back(2), last_block]
     me, x, z = place()
     loads = load_weights((query_ref, key_ref, value_ref), weight, local_sems)
     mine = pltpu.make_async_copy(
@@ -367,8 +365,11 @@
     if exchange:
         kept = pltpu.make_async_copy(grad_cols(me), heads_rows(me), local_sems.at[4])
         kept.start()
+    blocks[0]()
+    blocks[1]()
     relay_partner()
     relay_high()
+    blocks[2]()
     relay_low()
     if exchange:
         for step in range(1, 8):
@@ -380,6 +381,7 @@
     own_pair()
     project_rows(x, whole, weight, cos_ref, sin_ref, out_ref)
     relay_partner_low()
+    blocks[3]()
     relay_far()
     left_pair()
     project_rows((x + 3) % 4, whole, weight, cos_ref, sin_ref, out_ref)
@@ -395,30 +397,42 @@
     copies.finish()
 
 
-def gather_project(own, weights, cosines, sines, collective_id, grad=None):
+def gather_project(own, weights, cosines, sines, collective_id, grad=None, back=()):
     exchange = grad is not None
     vmem = pl.BlockSpec(memory_space=pltpu.VMEM)
     anywhere = pl.BlockSpec(memory_space=pl.ANY)
     count = GATHER_COPIES + (7 if exchange else 0)
     out_shape = [jax.ShapeDtypeStruct((1024, ALL_WIDE), jnp.bfloat16)]
     operands = [own, *weights, cosines, sines]
-    in_specs = [vmem, anywhere, anywhere, anywhere, vmem, vmem]
+    scratch = [
+        pltpu.VMEM((1024, COLS), jnp.bfloat16),
+        pltpu.VMEM((COLS, ALL_WIDE), jnp.bfloat16),
+        pltpu.SemaphoreType.DMA((5,)),
+        pltpu.SemaphoreType.DMA((count,)),
+        pltpu.SemaphoreType.DMA((count,)),
+    ]
     if exchange:
         out_shape.append(jax.ShapeDtypeStruct((1024, HEADS_WIDE), jnp.bfloat16))
         operands.append(grad)
-        in_specs.append(vmem)
+    else:
+        out_shape.append(jax.ShapeDtypeStruct((4, ALL_WIDE, 256), jnp.bfloat16))
+        operands.extend(back)
+        scratch.extend(
+            [
+                pltpu.VMEM((768, 256), jnp.float32),
+                pltpu.VMEM((HEAD_SIZE, 1024), jnp.bfloat16),
+                pltpu.VMEM((1024, HEAD_SIZE), jnp.float32),
+                pltpu.VMEM((1024, HEAD_SIZE), jnp.float32),
+            ]
+        )
+    in_specs = [vmem] * len(operands)
+    in_specs[1:4] = [anywhere] * 3
     return pl.pallas_call(
         functools.partial(gather_kernel, exchange),
         out_shape=out_shape,
         in_specs=in_specs,
         out_specs=[vmem] * len(out_shape),
-        scratch_shapes=[
-            pltpu.VMEM((1024, COLS), jnp.bfloat16),
-            pltpu.VMEM((COLS, ALL_WIDE), jnp.bfloat16),
-            pltpu.SemaphoreType.DMA((5,)),
-            pltpu.SemaphoreType.DMA((count,)),
-            pltpu.SemaphoreType.DMA((count,)),
-        ],
+        scratch_shapes=scratch,
         compiler_params=pltpu.CompilerParams(
             collective_id=collective_id, has_side_effects=True
         ),
@@ -440,7 +454,9 @@
     query_ref,
     key_ref,
     value_ref,
-    mixed_ref,
+    heads,
+    docs_col,
+    docs_row,
     sum_ref,
     owned_ref,
     weight,
@@ -455,6 +471,9 @@
     near_right_one,
     near_left_one,
     z_last,
+    bias,
+    value_turned,
+    mixed_ref,
     local_sems,
     send_sems,
     recv_sems,
@@ -471,10 +490,11 @@
     def mixed_rows(peer):
         return mixed_ref.at[pl.ds(pl.multiple_of(peer * ROWS, ROWS), ROWS), :]
 
-    kept = pltpu.make_async_copy(mixed_rows(me), owned_cols(me), local_sems.at[3])
-    kept.start()
     for one in loads:
         one.wait()
+
+    def attend(block):
+        attend_block(block, heads, docs_col, docs_row, bias, value_turned, mixed_ref)
 
     def share(xx, zz, offset, count):
         return shares.at[peer_of(xx, zz), pl.ds(offset, count), :]
@@ -501,7 +521,8 @@
     copies.send(6, pair_share(x + 1, 3072, 1024), near_right.at[:, pl.ds(1024, 1024), :], right)
     compute(3)
     copies.send(12, pair_share(x + 3, 2048, 1024), near_left.at[:, pl.ds(0, 1024), :], left)
-    compute(0)
+    value_turned[...] = heads[:, 640:768].astype(jnp.float32).T.astype(jnp.bfloat16)
+    attend(0)
     copies.arrived(5, far_right, left)
     for zz in range(2):
         spot = shares.at[2 * ((x + 1) % 4) + zz, pl.ds(2048, 1024), :]
@@ -512,14 +533,14 @@
         spot = shares.at[2 * ((x + 3) % 4) + zz, pl.ds(3072, 1024), :]
         add_rows(spot, [spot, far_left.at[zz]], 1024)
     copies.send(13, pair_share(x + 3, 3072, 1024), near_left.at[:, pl.ds(1024, 1024), :], left)
+    attend(1)
+    compute(0)
     copies.arrived(2, z_in.at[2], partner)
     spot = share(x + 2, z, 0, 2048)
     add_rows(spot, [spot, z_in.at[2]], 2048)
     copies.send(8, share(x + 2, z, 0, 1024), far_right_one, right)
     copies.send(14, share(x + 2, z, 1024, 1024), far_left_one, left)
-    for step in range(1, 8):
-        peer = (me + step) % 8
-        copies.send(16 + step, mixed_rows(peer), owned_cols(me), peer)
+    attend(2)
     copies.arrived(1, z_in.at[1], partner)
     spot = share(x + 1, z, 1024, 1024)
     add_rows(spot, [spot, z_in.at[1, pl.ds(1024, 1024), :]], 1024)
@@ -528,6 +549,12 @@
     spot = share(x + 3, z, 0, 1024)
     add_rows(spot, [spot, z_in.at[3, pl.ds(0, 1024), :]], 1024)
     copies.send(15, spot, near_left_one.at[pl.ds(0, 1024), :], left)
+    attend(3)
+    kept = pltpu.make_async_copy(mixed_rows(me), owned_cols(me), local_sems.at[3])
+    kept.start()
+    for step in range(1, 8):
+        peer = (me + step) % 8
+        copies.send(16 + step, mixed_rows(peer), owned_cols(me), peer)
     copies.arrived(8, far_right_one, left)
     spot = share(x + 1, z, 0, 1024)
     add_rows(spot, [spot, z_in.at[1, pl.ds(0, 1024), :], far_right_one], 1024)
@@ -568,7 +595,7 @@
     copies.finish()
 
 
-def reduce_project(turned, weights, mixed, collective_id):
+def reduce_project(turned, weights, heads, docs, collective_id):
     vmem = pl.BlockSpec(memory_space=pltpu.VMEM)
     anywhere = pl.BlockSpec(memory_space=pl.ANY)
     bf16 = jnp.bfloat16
@@ -578,7 +605,7 @@
             jax.ShapeDtypeStruct((ROWS, COLS), jnp.float32),
             jax.ShapeDtypeStruct((ROWS, COLS), bf16),
         ],
-        in_specs=[vmem, anywhere, anywhere, anywhere, vmem],
+        in_specs=[vmem, anywhere, anywhere, anywhere, vmem, vmem, vmem],
         out_specs=[vmem, vmem],
         scratch_shapes=[
             pltpu.VMEM((COLS, ALL_WIDE), bf16),
@@ -593,6 +620,9 @@
             pltpu.VMEM((2048, ROWS), bf16),
             pltpu.VMEM((2048, ROWS), bf16),
             pltpu.VMEM((2048, ROWS), bf16),
+            pltpu.VMEM((768, 256), jnp.float32),
+            pltpu.VMEM((HEAD_SIZE, 1024), bf16),
+            pltpu.VMEM((1024, HEADS_WIDE), bf16),
             pltpu.SemaphoreType.DMA((4,)),
             pltpu.SemaphoreType.DMA((24,)),
             pltpu.SemaphoreType.DMA((24,)),
@@ -600,7 +630,7 @@
         compiler_params=pltpu.CompilerParams(
             collective_id=collective_id, has_side_effects=True
         ),
-    )(turned, *weights, mixed)
+    )(turned, *weights, heads, *docs)
 
 
 def body(
@@ -627,28 +657,28 @@
     cosines, sines = rotation_tables(jnp.arange(8 * ROWS, dtype=jnp.float32))
     cos_wide = jnp.concatenate([cosines, cosines], 1)
     sin_wide = jnp.concatenate([-sines, sines], 1)
-    (forward_heads,) = gather_project(forward_normed, weights, cos_wide, sin_wide, 0)
-    mixed_rows = attend(
-        forward_heads[:, :512], forward_heads[:, 512:640], forward_heads[:, 640:], first_docs
-    )
     back_heads, head_gradients = gather_project(
         back_normed, weights, cos_wide, sin_wide, 1, output_grad[0]
     )
-    query_grad, key_grad, value_grad = attend_back(
-        back_heads[:, :512],
-        back_heads[:, 512:640],
-        back_heads[:, 640:],
-        head_gradients,
-        back_docs,
-        cosines,
-        sines,
-    )
-    turned = (
-        jnp.concatenate([query_grad, key_grad, value_grad], 1)
-        .reshape(4, 256, ALL_WIDE)
-        .transpose(0, 2, 1)
-    )
-    input_sum, owned_rows = reduce_project(turned, weights, mixed_rows, 2)
+    forward_heads, turned = gather_project(
+        forward_normed,
+        weights,
+        cos_wide,
+        sin_wide,
+        0,
+        None,
+        (
+            back_heads,
+            head_gradients,
+            back_docs[:, None],
+            back_docs[None, :],
+            cos_wide.T,
+            sin_wide.T,
+        ),
+    )
+    input_sum, owned_rows = reduce_project(
+        turned, weights, forward_heads, (first_docs[:, None], first_docs[None, :]), 2
+    )
     first_out = (forward_hidden + owned_rows.astype(jnp.float32)).astype(jnp.bfloat16)
     section_output = passed_along(first_out, "section", 1)
     gained = gain_row * input_sum

time: 347 us -> 261 us (0.75); the launches traced: 341 us -> 258 us
  matrix products: 36.3 us -> 0 us
  other arithmetic: 32.9 us -> 8.01 us
  local copies, waits for them, and re-layouts: 29.4 us -> 7.29 us
    dot_general x14 -> x0, matrix products: 36.3 us -> none  [the longest x4 8.8 us: block_probs(): jnp.einsum('tjgd,sjd->jgts', query_block, key_heads, preferred_element_ty...]
    concatenate x8 -> x0, other arithmetic: 7.96 us -> none  [the longest x1 2.25 us: body(): jnp.concatenate([query_grad, key_grad, value_grad], 1)]
    slice x5 -> x0, local copies, waits for them, and re-layouts: 6.49 us -> none  [the longest x1 2.24 us: attend_back(): query_block = query_head_count[begin_row:end_row]]
    reduce_sum x4 -> x0, other arithmetic: 6.3 us -> none  [block_probs(): return exp_scores / jnp.sum(exp_scores, axis=-1, keepdims=True)]
    reshape x2 -> x0, local copies, waits for them, and re-layouts: 5.05 us -> none  [the longest x1 2.59 us: body(): turned = jnp.concatenate([query_grad, key_grad, value_grad], 1).reshape(4...]
    another operation x4 -> x0, other arithmetic: 4.69 us -> none
    another operation x4 -> x0, local copies, waits for them, and re-layouts: 4.53 us -> none
where the time goes in v2:
time: 261 us; the launch traced here: 258 us
  Pallas kernels  221 us (85%)
  waiting for transfers between devices  11.7 us (4%)
  starting transfers between devices  9.79 us (4%)
  other arithmetic  8.01 us (3%)
  local copies, waits for them, and re-layouts  7.29 us (3%)
    pallas_call x2, Pallas kernels, gather_project(): pl.pallas_call(functools.partial(gather_kernel, exchange), out_shape=out_...  143 us
    pallas_call x1, Pallas kernels, reduce_project(): pl.pallas_call(reduce_kernel, out_shape=[jax.ShapeDtypeStruct((ROWS, COLS...  77.4 us
    ppermute x2, waiting for transfers between devices, passed_along(): return lax.ppermute(shard, axis, pairs)  11.7 us
    ppermute x2, starting transfers between devices, passed_along(): return lax.ppermute(shard, axis, pairs)  9.79 us
  transfers between devices with their start and end apart: 2, of which 2 were waited for; matrix products, arithmetic and copies ran while one was open for 0% of the time, Pallas kernels for 0%

profile of v2, /device:TPU:25, one launch (start us, length us, event | category | flops | bytes accessed | tf_op | source)
XLA Modules:
  0.0 258.1 jit_solution(1323318240440377820)
XLA Ops:
  0.6 1.0 fusion.15
  1.7 1.2 fusion.16
  2.9 1.0 copy.17.refs_4_
  3.9 1.0 copy.18.refs_5_
  4.9 0.3 fusion
  5.2 0.3 fusion.4
  5.5 0.8 constant_dynamic-slice_fusion
  6.3 1.1 copy.19.refs_8_
  7.4 1.1 copy.20.docs_col
  8.5 2.0 fusion.6
  10.5 78.3 %shard_map.104 = (bf16[1024,768]{1,0:T(8,128)(2,1)}, bf16[1024,512]{1,0:T(8,128)(2,1)}) custom-call(bf16[128,4096]{1,0:T(8,128)(2,1)} %get-tuple-element.18.refs_0_, bf16[4096,512]{1,0:T(8,128)(2,1)} %bitcast.25, bf16[4096,128]{1,0:T(8,128)(2,1)} %bitcast.28, bf16[4096,128]{1,0:T(8,128)(2,1)} %bitcast.31, f32[1024,128]{1,0:T(8,128)} %copy.17.refs_4_, ...), custom_call_target="tpu_custom_call" | custom-call | tf_op jit(solution)/shard_map/pallas_call | solution.py:430
  88.8 64.8 %shard_map.105 = (bf16[1024,768]{1,0:T(8,128)(2,1)}, bf16[4,768,256]{2,1,0:T(8,128)(2,1)}) custom-call(bf16[128,4096]{1,0:T(8,128)(2,1)} %get-tuple-element.19.refs_0_, bf16[4096,512]{1,0:T(8,128)(2,1)} %bitcast.26, bf16[4096,128]{1,0:T(8,128)(2,1)} %bitcast.29, bf16[4096,128]{1,0:T(8,128)(2,1)} %bitcast.32, f32[1024,128]{1,0:T(8,128)} %copy.17.refs_4_, ...), custom_call_target="tpu_custom_call" | custom-call | tf_op jit(solution)/shard_map/pallas_call | solution.py:430
  153.6 77.4 %shard_map.106 = (f32[128,4096]{1,0:T(8,128)}, bf16[128,4096]{1,0:T(8,128)(2,1)}) custom-call(bf16[4,768,256]{2,1,0:T(8,128)(2,1)} %get-tuple-element.10.turned, bf16[4096,512]{1,0:T(8,128)(2,1)} %bitcast.27, bf16[4096,128]{1,0:T(8,128)(2,1)} %bitcast.30, bf16[4096,128]{1,0:T(8,128)(2,1)} %bitcast.33, bf16[1024,768]{1,0:T(8,128)(2,1)} %get-tuple-element.11.heads, ...), custom_call_target="tpu_custom_call" | custom-call | tf_op jit(solution)/shard_map/pallas_call | solution.py:602
  231.0 2.1 fusion.12
  233.1 0.1 copy-done.2
  233.2 0.3 copy-done.3
  233.5 0.9 fusion.11
  234.4 5.0 %collective-permute-start.1 = (bf16[128,4096]{1,0:T(8,128)(2,1)S(1)}, bf16[128,4096]{1,0:T(8,128)(2,1)S(1)}, u32[]{:S(2)}, u32[]{:S(2)}) collective-permute-start(bf16[128,4096]{1,0:T(8,128)(2,1)S(1)} %fusion.11), channel_id=1, source_target_pairs={{8,0},{16,8},{24,16},{32,24},{40,32},{48,40},{56,48},{64,56},{72,6... | collective-permute-start | bytes 3145736 | tf_op jit(solution)/shard_map/ppermute | solution.py:27
  239.4 0.2 fusion.3
  239.7 4.8 %collective-permute-start = (bf16[128,4096]{1,0:T(8,128)(2,1)S(1)}, bf16[128,4096]{1,0:T(8,128)(2,1)S(1)}, u32[]{:S(2)}, u32[]{:S(2)}) collective-permute-start(bf16[128,4096]{1,0:T(8,128)(2,1)S(1)} %fusion.3), channel_id=1, source_target_pairs={{0,8},{8,16},{16,24},{24,32},{32,40},{40,48},{48,56},{56,64},{64,7... | collective-permute-start | bytes 3145736 | tf_op jit(solution)/shard_map/ppermute | solution.py:27
  244.5 10.3 %collective-permute-done.1 = bf16[128,4096]{1,0:T(8,128)(2,1)S(1)} collective-permute-done((bf16[128,4096]{1,0:T(8,128)(2,1)S(1)}, bf16[128,4096]{1,0:T(8,128)(2,1)S(1)}, u32[]{:S(2)}, u32[]{:S(2)}) %collective-permute-start.1) | collective-permute-done | bytes 1048608 | tf_op jit(solution)/shard_map/ppermute | solution.py:27
  254.7 1.4 collective-permute-done
  256.2 1.0 copy.23
  257.1 1.0 copy.24
  (16 shorter events, 0.1 us)
Async XLA Ops:
  1.7 3.3 %copy-start.1 = (bf16[1,128,4096]{2,1,0:T(8,128)(2,1)S(1)}, bf16[1,128,4096]{2,1,0:T(8,128)(2,1)}, u32[]{:S(2)}) copy-start(bf16[1,128,4096]{2,1,0:T(8,128)(2,1)} %param.9) | copy-start | bytes 3145732
  2.9 2.3 copy-start
  3.9 4.6 %copy-start.5 = (f32[1,4096]{1,0:T(1,128)S(1)}, f32[1,4096]{1,0:T(1,128)}, u32[]{:S(2)}) copy-start(f32[1,4096]{1,0:T(1,128)} %param.14) | copy-start | bytes 49156
  6.3 4.1 %copy-start.6 = (s32[1,1024]{1,0:T(1,128)}, s32[1,1024]{1,0:T(1,128)S(1)}, u32[]{:S(2)}) copy-start(s32[1,1024]{1,0:T(1,128)S(1)} %get-tuple-element.28.docs_row) | copy-start | bytes 12292
  6.3 4.1 %copy-start.7 = (s32[1,1024]{1,0:T(1,128)}, s32[1,1024]{1,0:T(1,128)S(1)}, u32[]{:S(2)}) copy-start(s32[1,1024]{1,0:T(1,128)S(1)} %get-tuple-element.29.refs_9_) | copy-start | bytes 12292
  231.0 2.2 copy-start.2
  231.0 2.5 copy-start.3
  233.5 5.9 %copy-start.4 = (bf16[128,4096]{1,0:T(8,128)(2,1)S(1)}, bf16[128,4096]{1,0:T(8,128)(2,1)}, u32[]{:S(2)}) copy-start(bf16[128,4096]{1,0:T(8,128)(2,1)} %get-tuple-element.12) | copy-start | bytes 3145732
  234.4 20.3 %collective-permute-start.1 = (bf16[128,4096]{1,0:T(8,128)(2,1)S(1)}, bf16[128,4096]{1,0:T(8,128)(2,1)S(1)}, u32[]{:S(2)}, u32[]{:S(2)}) collective-permute-start(bf16[128,4096]{1,0:T(8,128)(2,1)S(1)} %fusion.11), channel_id=1, source_target_pairs={{8,0},{16,8},{24,16},{32,24},{40,32},{48,40},{56,48},{64,56},{72,6... | collective-permute-start | bytes 3145736 | tf_op jit(solution)/shard_map/ppermute | solution.py:27
  239.7 16.5 %collective-permute-start = (bf16[128,4096]{1,0:T(8,128)(2,1)S(1)}, bf16[128,4096]{1,0:T(8,128)(2,1)S(1)}, u32[]{:S(2)}, u32[]{:S(2)}) collective-permute-start(bf16[128,4096]{1,0:T(8,128)(2,1)S(1)} %fusion.3), channel_id=1, source_target_pairs={{0,8},{8,16},{16,24},{24,32},{32,40},{40,48},{48,56},{56,64},{64,7... | collective-permute-start | bytes 3145736 | tf_op jit(solution)/shard_map/ppermute | solution.py:27

commit v3 on v2

--- a/solution.py
+++ b/solution.py
@@ -1,4 +1,4 @@
-import functools
+import types
 
 import jax
 import jax.numpy as jnp
@@ -133,16 +133,16 @@
 
 
 class Copies:
-    def __init__(self, send_sems, recv_sems):
-        self.send_sems, self.recv_sems = send_sems, recv_sems
+    def __init__(self, send_sems, recv_sems, base):
+        self.send_sems, self.recv_sems, self.base = send_sems, recv_sems, base
         self.sent = []
 
     def copy(self, number, src, dst, peer):
         return pltpu.make_async_remote_copy(
             src_ref=src,
             dst_ref=dst,
-            send_sem=self.send_sems.at[number],
-            recv_sem=self.recv_sems.at[number],
+            send_sem=self.send_sems.at[self.base + number],
+            recv_sem=self.recv_sems.at[self.base + number],
             device_id={"seq": peer},
             device_id_type=MESH,
         )
@@ -200,7 +200,7 @@
         )
 
 
-def gather_plan(copies, own, whole):
+def gather_steps(copies, own, whole):
     me, x, z = place()
     right, left, partner = peer_of(x + 1, z), peer_of(x + 3, z), peer_of(x, 1 - z)
 
@@ -274,169 +274,18 @@
         got(4, partner, x + 2, 1 - z, 64, 32)
         got(5, partner, x + 2, 1 - z, 96, 32)
 
-    return (
-        begin,
-        relay_partner,
-        relay_high,
-        relay_low,
-        own_pair,
-        relay_far,
-        relay_partner_low,
-        left_pair,
-        right_pair,
-        far_pair,
+    return types.SimpleNamespace(
+        begin=begin,
+        relay_partner=relay_partner,
+        relay_high=relay_high,
+        relay_low=relay_low,
+        own_pair=own_pair,
+        relay_far=relay_far,
+        relay_partner_low=relay_partner_low,
+        left_pair=left_pair,
+        right_pair=right_pair,
+        far_pair=far_pair,
     )
-
-
-GATHER_COPIES = 18
-
-
-def gather_kernel(exchange, *refs):
-    own, query_ref, key_ref, value_ref, cos_ref, sin_ref = refs[:6]
-    refs = refs[6:]
-    if exchange:
-        grad_ref, out_ref, heads_ref, whole, weight, local_sems, send_sems, recv_sems = refs
-        blocks = [lambda: None] * 4
-    else:
-        back_heads, back_grads, docs_col, docs_row, cos_turned, sin_turned = refs[:6]
-        out_ref, back_out, whole, weight, local_sems, send_sems, recv_sems = refs[6:13]
-        bias, key_turned, key_grad, value_grad = refs[13:]
-
-        def back(block):
-            attend_back_block(
-                block,
-                back_heads,
-                back_grads,
-                docs_col,
-                docs_row,
-                cos_turned,
-                sin_turned,
-                bias,
-                key_turned,
-                key_grad,
-                value_grad,
-                back_out,
-            )
-
-        def first_block():
-            key_turned[...] = back_heads[:, 512:640].astype(jnp.float32).T.astype(jnp.bfloat16)
-            key_grad[...] = jnp.zeros_like(key_grad)
-            value_grad[...] = jnp.zeros_like(value_grad)
-            back(0)
-
-        def last_block():
-            back(3)
-            for block in range(4):
-                finish_back(block, cos_ref, sin_ref, key_grad, value_grad, back_out)
-
-        blocks = [first_block, lambda: back(1), lambda: back(2), last_block]
-    me, x, z = place()
-    loads = load_weights((query_ref, key_ref, value_ref), weight, local_sems)
-    mine = pltpu.make_async_copy(
-        own, whole.at[pl.ds(pl.multiple_of(me * ROWS, ROWS), ROWS), :], local_sems.at[3]
-    )
-    mine.start()
-    if exchange:
-        peers = [(me + step) % 8 for step in range(1, 8)]
-    else:
-        peers = [peer_of(x + 1, z), peer_of(x + 3, z), peer_of(x, 1 - z)]
-    greet(peers)
-    copies = Copies(send_sems, recv_sems)
-    (
-        begin,
-        relay_partner,
-        relay_high,
-        relay_low,
-        own_pair,
-        relay_far,
-        relay_partner_low,
-        left_pair,
-        right_pair,
-        far_pair,
-    ) = gather_plan(copies, own, whole)
-    begin()
-
-    def heads_rows(peer):
-        return heads_ref.at[pl.ds(pl.multiple_of(peer * ROWS, ROWS), ROWS), :]
-
-    def grad_cols(peer):
-        return grad_ref.at[:, pl.ds(pl.multiple_of(peer * HEADS_WIDE, HEADS_WIDE), HEADS_WIDE)]
-
-    if exchange:
-        kept = pltpu.make_async_copy(grad_cols(me), heads_rows(me), local_sems.at[4])
-        kept.start()
-    blocks[0]()
-    blocks[1]()
-    relay_partner()
-    relay_high()
-    blocks[2]()
-    relay_low()
-    if exchange:
-        for step in range(1, 8):
-            peer = (me + step) % 8
-            copies.send(GATHER_COPIES + step - 1, grad_cols(peer), heads_rows(me), peer)
-    for one in loads:
-        one.wait()
-    mine.wait()
-    own_pair()
-    project_rows(x, whole, weight, cos_ref, sin_ref, out_ref)
-    relay_partner_low()
-    blocks[3]()
-    relay_far()
-    left_pair()
-    project_rows((x + 3) % 4, whole, weight, cos_ref, sin_ref, out_ref)
-    right_pair()
-    project_rows((x + 1) % 4, whole, weight, cos_ref, sin_ref, out_ref)
-    far_pair()
-    project_rows((x + 2) % 4, whole, weight, cos_ref, sin_ref, out_ref)
-    if exchange:
-        kept.wait()
-        for step in range(1, 8):
-            peer = (me + 8 - step) % 8
-            copies.arrived(GATHER_COPIES + step - 1, heads_rows(peer), peer)
-    copies.finish()
-
-
-def gather_project(own, weights, cosines, sines, collective_id, grad=None, back=()):
-    exchange = grad is not None
-    vmem = pl.BlockSpec(memory_space=pltpu.VMEM)
-    anywhere = pl.BlockSpec(memory_space=pl.ANY)
-    count = GATHER_COPIES + (7 if exchange else 0)
-    out_shape = [jax.ShapeDtypeStruct((1024, ALL_WIDE), jnp.bfloat16)]
-    operands = [own, *weights, cosines, sines]
-    scratch = [
-        pltpu.VMEM((1024, COLS), jnp.bfloat16),
-        pltpu.VMEM((COLS, ALL_WIDE), jnp.bfloat16),
-        pltpu.SemaphoreType.DMA((5,)),
-        pltpu.SemaphoreType.DMA((count,)),
-        pltpu.SemaphoreType.DMA((count,)),
-    ]
-    if exchange:
-        out_shape.append(jax.ShapeDtypeStruct((1024, HEADS_WIDE), jnp.bfloat16))
-        operands.append(grad)
-    else:
-        out_shape.append(jax.ShapeDtypeStruct((4, ALL_WIDE, 256), jnp.bfloat16))
-        operands.extend(back)
-        scratch.extend(
-            [
-                pltpu.VMEM((768, 256), jnp.float32),
-                pltpu.VMEM((HEAD_SIZE, 1024), jnp.bfloat16),
-                pltpu.VMEM((1024, HEAD_SIZE), jnp.float32),
-                pltpu.VMEM((1024, HEAD_SIZE), jnp.float32),
-            ]
-        )
-    in_specs = [vmem] * len(operands)
-    in_specs[1:4] = [anywhere] * 3
-    return pl.pallas_call(
-        functools.partial(gather_kernel, exchange),
-        out_shape=out_shape,
-        in_specs=in_specs,
-        out_specs=[vmem] * len(out_shape),
-        scratch_shapes=scratch,
-        compiler_params=pltpu.CompilerParams(
-            collective_id=collective_id, has_side_effects=True
-        ),
-    )(*operands)
 
 
 def add_rows(out, terms, count, chunk=256):
@@ -449,17 +298,36 @@
         out[rows, :] = total.astype(jnp.bfloat16)
 
 
-def reduce_kernel(
-    turned,
+def tick_kernel(
+    own_back,
+    own_forward,
+    grad_ref,
     query_ref,
     key_ref,
     value_ref,
-    heads,
-    docs_col,
-    docs_row,
+    cos_ref,
+    sin_ref,
+    cos_turned,
+    sin_turned,
+    back_col,
+    back_row,
+    forward_col,
+    forward_row,
     sum_ref,
     owned_ref,
+    whole_back,
+    whole_forward,
     weight,
+    back_heads,
+    heads,
+    back_grads,
+    turned,
+    bias,
+    key_turned,
+    key_grad,
+    value_grad,
+    value_turned,
+    mixed_ref,
     shares,
     z_in,
     far_right,
@@ -471,30 +339,91 @@
     near_right_one,
     near_left_one,
     z_last,
-    bias,
-    value_turned,
-    mixed_ref,
     local_sems,
     send_sems,
     recv_sems,
 ):
     me, x, z = place()
+    right, left, partner = peer_of(x + 1, z), peer_of(x + 3, z), peer_of(x, 1 - z)
     loads = load_weights((query_ref, key_ref, value_ref), weight, local_sems)
-    greet([(me + step) % 8 for step in range(1, 8)])
-    copies = Copies(send_sems, recv_sems)
-    right, left, partner = peer_of(x + 1, z), peer_of(x + 3, z), peer_of(x, 1 - z)
-
-    def owned_cols(peer):
-        return owned_ref.at[:, pl.ds(pl.multiple_of(peer * HEADS_WIDE, HEADS_WIDE), HEADS_WIDE)]
-
-    def mixed_rows(peer):
-        return mixed_ref.at[pl.ds(pl.multiple_of(peer * ROWS, ROWS), ROWS), :]
-
-    for one in loads:
+
+    def wide_rows(ref, peer):
+        return ref.at[pl.ds(pl.multiple_of(peer * ROWS, ROWS), ROWS), :]
+
+    def wide_cols(ref, peer):
+        return ref.at[:, pl.ds(pl.multiple_of(peer * HEADS_WIDE, HEADS_WIDE), HEADS_WIDE)]
+
+    kept = [
+        pltpu.make_async_copy(own_back, wide_rows(whole_back, me), local_sems.at[3]),
+        pltpu.make_async_copy(own_forward, wide_rows(whole_forward, me), local_sems.at[4]),
+        pltpu.make_async_copy(wide_cols(grad_ref, me), wide_rows(back_grads, me), local_sems.at[5]),
+    ]
+    for one in kept:
+        one.start()
+    others = [(me + step) % 8 for step in range(1, 8)]
+    sources = [(me + 8 - step) % 8 for step in range(1, 8)]
+    greet(others)
+    back_copies = Copies(send_sems, recv_sems, 0)
+    forward_copies = Copies(send_sems, recv_sems, 18)
+    grad_copies = Copies(send_sems, recv_sems, 36)
+    mixed_copies = Copies(send_sems, recv_sems, 43)
+    copies = Copies(send_sems, recv_sems, 50)
+    back = gather_steps(back_copies, own_back, whole_back)
+    forward = gather_steps(forward_copies, own_forward, whole_forward)
+
+    def project(pair, whole, out):
+        project_rows(pair % 4, whole, weight, cos_ref, sin_ref, out)
+
+    back.begin()
+    back.relay_partner()
+    back.relay_high()
+    back.relay_low()
+    for number, peer in enumerate(others):
+        grad_copies.send(number, wide_cols(grad_ref, peer), wide_rows(back_grads, me), peer)
+    for one in loads + kept:
         one.wait()
-
-    def attend(block):
-        attend_block(block, heads, docs_col, docs_row, bias, value_turned, mixed_ref)
+    back.own_pair()
+    project(x, whole_back, back_heads)
+    back.relay_partner_low()
+    back.relay_far()
+    forward.begin()
+    back.left_pair()
+    project(x + 3, whole_back, back_heads)
+    back.right_pair()
+    project(x + 1, whole_back, back_heads)
+    back.far_pair()
+    project(x + 2, whole_back, back_heads)
+    for number, peer in enumerate(sources):
+        grad_copies.arrived(number, wide_rows(back_grads, peer), peer)
+
+    def back_block(block):
+        attend_back_block(
+            block,
+            back_heads,
+            back_grads,
+            back_col,
+            back_row,
+            cos_turned,
+            sin_turned,
+            bias,
+            key_turned,
+            key_grad,
+            value_grad,
+            turned,
+        )
+
+    key_turned[...] = back_heads[:, 512:640].astype(jnp.float32).T.astype(jnp.bfloat16)
+    key_grad[...] = jnp.zeros_like(key_grad)
+    value_grad[...] = jnp.zeros_like(value_grad)
+    back_block(0)
+    back_block(1)
+    forward.relay_partner()
+    forward.relay_high()
+    back_block(2)
+    forward.relay_low()
+    back_block(3)
+    for block in range(4):
+        finish_back(block, cos_ref, sin_ref, key_grad, value_grad, turned)
 
     def share(xx, zz, offset, count):
         return shares.at[peer_of(xx, zz), pl.ds(offset, count), :]
@@ -512,15 +441,35 @@
             shares[2 * pair, rows, :] = product[:, :128].astype(jnp.bfloat16)
             shares[2 * pair + 1, rows, :] = product[:, 128:].astype(jnp.bfloat16)
 
+    def attend(block):
+        attend_block(block, heads, forward_col, forward_row, bias, value_turned, mixed_ref)
+
+    compute(2)
+    compute(1)
+    forward.own_pair()
+    forward.relay_partner_low()
+    forward.relay_far()
+
+    def send_along_z(delta):
         copies.send(delta, share(x + delta, 1 - z, 0, 2048), z_in.at[delta], partner)
 
-    compute(2)
     copies.send(5, pair_share(x + 2, 2048, 1024), far_right, right)
     copies.send(11, pair_share(x + 2, 3072, 1024), far_left, left)
-    compute(1)
+    send_along_z(2)
     copies.send(6, pair_share(x + 1, 3072, 1024), near_right.at[:, pl.ds(1024, 1024), :], right)
+    send_along_z(1)
     compute(3)
     copies.send(12, pair_share(x + 3, 2048, 1024), near_left.at[:, pl.ds(0, 1024), :], left)
+    send_along_z(3)
+    compute(0)
+    send_along_z(0)
+    project(x, whole_forward, heads)
+    forward.left_pair()
+    project(x + 3, whole_forward, heads)
+    forward.right_pair()
+    project(x + 1, whole_forward, heads)
+    forward.far_pair()
+    project(x + 2, whole_forward, heads)
     value_turned[...] = heads[:, 640:768].astype(jnp.float32).T.astype(jnp.bfloat16)
     attend(0)
     copies.arrived(5, far_right, left)
@@ -534,7 +483,6 @@
         add_rows(spot, [spot, far_left.at[zz]], 1024)
     copies.send(13, pair_share(x + 3, 3072, 1024), near_left.at[:, pl.ds(1024, 1024), :], left)
     attend(1)
-    compute(0)
     copies.arrived(2, z_in.at[2], partner)
     spot = share(x + 2, z, 0, 2048)
     add_rows(spot, [spot, z_in.at[2]], 2048)
@@ -550,11 +498,12 @@
     add_rows(spot, [spot, z_in.at[3, pl.ds(0, 1024), :]], 1024)
     copies.send(15, spot, near_left_one.at[pl.ds(0, 1024), :], left)
     attend(3)
-    kept = pltpu.make_async_copy(mixed_rows(me), owned_cols(me), local_sems.at[3])
-    kept.start()
-    for step in range(1, 8):
-        peer = (me + step) % 8
-        copies.send(16 + step, mixed_rows(peer), owned_cols(me), peer)
+    kept_mixed = pltpu.make_async_copy(
+        wide_rows(mixed_ref, me), wide_cols(owned_ref, me), local_sems.at[6]
+    )
+    kept_mixed.start()
+    for number, peer in enumerate(others):
+        mixed_copies.send(number, wide_rows(mixed_ref, peer), wide_cols(owned_ref, me), peer)
     copies.arrived(8, far_right_one, left)
     spot = share(x + 1, z, 0, 1024)
     add_rows(spot, [spot, z_in.at[1, pl.ds(0, 1024), :], far_right_one], 1024)
@@ -586,29 +535,44 @@
     copies.arrived(10, near_right_one.at[pl.ds(0, 1024), :], left)
     copies.arrived(16, near_left_one.at[pl.ds(1024, 1024), :], right)
     total([share(x, z, 0, 2048), z_in.at[0], near_right_one, near_left_one], 0)
-    kept.wait()
-    for step in range(1, 8):
-        peer = (me + 8 - step) % 8
-        copies.arrived(16 + step, owned_cols(peer), peer)
+    kept_mixed.wait()
+    for number, peer in enumerate(sources):
+        mixed_copies.arrived(number, wide_cols(owned_ref, peer), peer)
     copies.arrived(4, z_last, partner)
     total([share(x, z, 2048, 2048), near_right.at[z], near_left.at[z], z_last], 2048)
-    copies.finish()
-
-
-def reduce_project(turned, weights, heads, docs, collective_id):
+    for each in (back_copies, forward_copies, grad_copies, mixed_copies, copies):
+        each.finish()
+
+
+def tick(operands, weights):
     vmem = pl.BlockSpec(memory_space=pltpu.VMEM)
     anywhere = pl.BlockSpec(memory_space=pl.ANY)
-    bf16 = jnp.bfloat16
+    bf16, f32 = jnp.bfloat16, jnp.float32
+    all_operands = [*operands[:3], *weights, *operands[3:]]
+    in_specs = [vmem] * len(all_operands)
+    in_specs[3:6] = [anywhere] * 3
     return pl.pallas_call(
-        reduce_kernel,
+        tick_kernel,
         out_shape=[
-            jax.ShapeDtypeStruct((ROWS, COLS), jnp.float32),
+            jax.ShapeDtypeStruct((ROWS, COLS), f32),
             jax.ShapeDtypeStruct((ROWS, COLS), bf16),
         ],
-        in_specs=[vmem, anywhere, anywhere, anywhere, vmem, vmem, vmem],
+        in_specs=in_specs,
         out_specs=[vmem, vmem],
         scratch_shapes=[
+            pltpu.VMEM((1024, COLS), bf16),
+            pltpu.VMEM((1024, COLS), bf16),
             pltpu.VMEM((COLS, ALL_WIDE), bf16),
+            pltpu.VMEM((1024, ALL_WIDE), bf16),
+            pltpu.VMEM((1024, ALL_WIDE), bf16),
+            pltpu.VMEM((1024, HEADS_WIDE), bf16),
+            pltpu.VMEM((4, ALL_WIDE, 256), bf16),
+            pltpu.VMEM((768, 256), f32),
+            pltpu.VMEM((HEAD_SIZE, 1024), bf16),
+            pltpu.VMEM((1024, HEAD_SIZE), f32),
+            pltpu.VMEM((1024, HEAD_SIZE), f32),
+            pltpu.VMEM((HEAD_SIZE, 1024), bf16),
+            pltpu.VMEM((1024, HEADS_WIDE), bf16),
             pltpu.VMEM((8, COLS, ROWS), bf16),
             pltpu.VMEM((4, 2048, ROWS), bf16),
             pltpu.VMEM((2, 1024, ROWS), bf16),
@@ -620,17 +584,14 @@
             pltpu.VMEM((2048, ROWS), bf16),
             pltpu.VMEM((2048, ROWS), bf16),
             pltpu.VMEM((2048, ROWS), bf16),
-            pltpu.VMEM((768, 256), jnp.float32),
-            pltpu.VMEM((HEAD_SIZE, 1024), bf16),
-            pltpu.VMEM((1024, HEADS_WIDE), bf16),
-            pltpu.SemaphoreType.DMA((4,)),
-            pltpu.SemaphoreType.DMA((24,)),
-            pltpu.SemaphoreType.DMA((24,)),
+            pltpu.SemaphoreType.DMA((7,)),
+            pltpu.SemaphoreType.DMA((67,)),
+            pltpu.SemaphoreType.DMA((67,)),
         ],
         compiler_params=pltpu.CompilerParams(
-            collective_id=collective_id, has_side_effects=True
+            collective_id=0, has_side_effects=True, vmem_limit_bytes=66000000
         ),
-    )(turned, *weights, heads, *docs)
+    )(*all_operands)
 
 
 def body(
@@ -657,27 +618,21 @@
     cosines, sines = rotation_tables(jnp.arange(8 * ROWS, dtype=jnp.float32))
     cos_wide = jnp.concatenate([cosines, cosines], 1)
     sin_wide = jnp.concatenate([-sines, sines], 1)
-    back_heads, head_gradients = gather_project(
-        back_normed, weights, cos_wide, sin_wide, 1, output_grad[0]
-    )
-    forward_heads, turned = gather_project(
-        forward_normed,
-        weights,
-        cos_wide,
-        sin_wide,
-        0,
-        None,
+    input_sum, owned_rows = tick(
         (
-            back_heads,
-            head_gradients,
+            back_normed,
+            forward_normed,
+            output_grad[0],
+            cos_wide,
+            sin_wide,
+            cos_wide.T,
+            sin_wide.T,
             back_docs[:, None],
             back_docs[None, :],
-            cos_wide.T,
-            sin_wide.T,
+            first_docs[:, None],
+            first_docs[None, :],
         ),
-    )
-    input_sum, owned_rows = reduce_project(
-        turned, weights, forward_heads, (first_docs[:, None], first_docs[None, :]), 2
+        weights,
     )
     first_out = (forward_hidden + owned_rows.astype(jnp.float32)).astype(jnp.bfloat16)
     section_output = passed_along(first_out, "section", 1)

time: 261 us -> 246 us (0.943)
  Pallas kernels: 221 us -> 202 us
  other arithmetic: 8.01 us -> 12.1 us
    pallas_call x3 -> x1, Pallas kernels: 221 us -> 202 us  [tick(): pl.pallas_call(tick_kernel, out_shape=[jax.ShapeDtypeStruct((ROWS, COLS),...]
where the time goes in v3:
time: 246 us; the launch traced here: 243 us
  Pallas kernels  202 us (82%)
  other arithmetic  12.1 us (5%)
  waiting for transfers between devices  11.7 us (5%)
  starting transfers between devices  9.18 us (4%)
  local copies, waits for them, and re-layouts  7.33 us (3%)
    pallas_call x1, Pallas kernels, tick(): pl.pallas_call(tick_kernel, out_shape=[jax.ShapeDtypeStruct((ROWS, COLS),...  202 us
    ppermute x2, waiting for transfers between devices, passed_along(): return lax.ppermute(shard, axis, pairs)  11.7 us
    ppermute x2, starting transfers between devices, passed_along(): return lax.ppermute(shard, axis, pairs)  9.18 us
  transfers between devices with their start and end apart: 2, of which 2 were waited for; matrix products, arithmetic and copies ran while one was open for 0% of the time, Pallas kernels for 0%

profile of v3, /device:TPU:25, one launch (start us, length us, event | category | flops | bytes accessed | tf_op | source)
XLA Modules:
  0.0 243.4 jit_solution(15461475403473561684)
XLA Ops:
  0.7 1.5 fusion
  2.2 1.5 fusion.4
  3.7 0.8 constant_dynamic-slice_fusion
  4.5 1.1 copy.15.back_col
  5.6 1.0 copy.16.forward_col
  6.6 1.0 fusion.15
  7.6 0.0 copy-start.2
  7.6 0.0 copy-start.6
  7.6 1.2 fusion.16
  8.9 1.0 copy.13.cos_ref
  9.9 1.0 copy.14.sin_ref
  10.9 2.0 fusion.2
  12.9 202.3 %shard_map.104 = (f32[128,4096]{1,0:T(8,128)}, bf16[128,4096]{1,0:T(8,128)(2,1)}) custom-call(bf16[128,4096]{1,0:T(8,128)(2,1)} %get-tuple-element.11.own_back, bf16[128,4096]{1,0:T(8,128)(2,1)} %get-tuple-element.10.own_forward, bf16[128,4096]{1,0:T(8,128)(2,1)} %bitcast.26, bf16[4096,512]{1,0:T(8,128)(2,1)} %bitcast.25, bf16[4096,128]{1,0:T(8,128)(2,1)} %bitcast.29, ...), custom_call_target="tpu_custom_call" | custom-call | tf_op jit(solution)/shard_map/pallas_call | solution.py:554
  215.2 0.0 copy-start.1
  215.2 2.4 fusion.12
  217.6 0.5 copy-done.4
  218.1 2.2 fusion.11
  220.3 3.5 %collective-permute-start.1 = (bf16[128,4096]{1,0:T(8,128)(2,1)S(1)}, bf16[128,4096]{1,0:T(8,128)(2,1)S(1)}, u32[]{:S(2)}, u32[]{:S(2)}) collective-permute-start(bf16[128,4096]{1,0:T(8,128)(2,1)S(1)} %fusion.11), channel_id=1, source_target_pairs={{8,0},{16,8},{24,16},{32,24},{40,32},{48,40},{56,48},{64,56},{72,6... | collective-permute-start | bytes 3145736 | tf_op jit(solution)/shard_map/ppermute | solution.py:27
  223.8 0.2 fusion.3
  224.1 5.7 %collective-permute-start = (bf16[128,4096]{1,0:T(8,128)(2,1)S(1)}, bf16[128,4096]{1,0:T(8,128)(2,1)S(1)}, u32[]{:S(2)}, u32[]{:S(2)}) collective-permute-start(bf16[128,4096]{1,0:T(8,128)(2,1)S(1)} %fusion.3), channel_id=1, source_target_pairs={{0,8},{8,16},{16,24},{24,32},{32,40},{40,48},{48,56},{56,64},{64,7... | collective-permute-start | bytes 3145736 | tf_op jit(solution)/shard_map/ppermute | solution.py:27
  229.8 10.3 %collective-permute-done.1 = bf16[128,4096]{1,0:T(8,128)(2,1)S(1)} collective-permute-done((bf16[128,4096]{1,0:T(8,128)(2,1)S(1)}, bf16[128,4096]{1,0:T(8,128)(2,1)S(1)}, u32[]{:S(2)}, u32[]{:S(2)}) %collective-permute-start.1) | collective-permute-done | bytes 1048608 | tf_op jit(solution)/shard_map/ppermute | solution.py:27
  240.0 1.5 collective-permute-done
  241.5 1.0 copy.19
  242.5 1.0 copy.20
  (16 shorter events, 0.0 us)
Async XLA Ops:
  4.5 4.4 %copy-start.7 = (s32[1,1024]{1,0:T(1,128)}, s32[1,1024]{1,0:T(1,128)S(1)}, u32[]{:S(2)}) copy-start(s32[1,1024]{1,0:T(1,128)S(1)} %get-tuple-element.20.forward_row) | copy-start | bytes 12292
  4.5 4.4 %copy-start.8 = (s32[1,1024]{1,0:T(1,128)}, s32[1,1024]{1,0:T(1,128)S(1)}, u32[]{:S(2)}) copy-start(s32[1,1024]{1,0:T(1,128)S(1)} %get-tuple-element.21.back_row) | copy-start | bytes 12292
  7.6 3.3 %copy-start = (bf16[1,128,4096]{2,1,0:T(8,128)(2,1)S(1)}, bf16[1,128,4096]{2,1,0:T(8,128)(2,1)}, u32[]{:S(2)}) copy-start(bf16[1,128,4096]{2,1,0:T(8,128)(2,1)} %param.10) | copy-start | bytes 3145732
  7.6 3.3 %copy-start.2 = (bf16[1,128,4096]{2,1,0:T(8,128)(2,1)S(1)}, bf16[1,128,4096]{2,1,0:T(8,128)(2,1)}, u32[]{:S(2)}) copy-start(bf16[1,128,4096]{2,1,0:T(8,128)(2,1)} %param.9) | copy-start | bytes 3145732
  7.6 3.3 %copy-start.6 = (f32[1,4096]{1,0:T(1,128)S(1)}, f32[1,4096]{1,0:T(1,128)}, u32[]{:S(2)}) copy-start(f32[1,4096]{1,0:T(1,128)} %param.14) | copy-start | bytes 49156
  215.2 2.4 copy-start.1
  215.2 2.9 %copy-start.4 = (f32[128,4096]{1,0:T(8,128)S(1)}, f32[128,4096]{1,0:T(8,128)}, u32[]{:S(2)}) copy-start(f32[128,4096]{1,0:T(8,128)} %get-tuple-element.5) | copy-start | bytes 6291460
  218.1 5.7 %copy-start.3 = (bf16[1,128,4096]{2,1,0:T(8,128)(2,1)S(1)}, bf16[1,128,4096]{2,1,0:T(8,128)(2,1)}, u32[]{:S(2)}) copy-start(bf16[1,128,4096]{2,1,0:T(8,128)(2,1)} %param.9) | copy-start | bytes 3145732
  218.1 5.7 %copy-start.5 = (bf16[128,4096]{1,0:T(8,128)(2,1)S(1)}, bf16[128,4096]{1,0:T(8,128)(2,1)}, u32[]{:S(2)}) copy-start(bf16[128,4096]{1,0:T(8,128)(2,1)} %get-tuple-element.4) | copy-start | bytes 3145732
  220.3 19.7 %collective-permute-start.1 = (bf16[128,4096]{1,0:T(8,128)(2,1)S(1)}, bf16[128,4096]{1,0:T(8,128)(2,1)S(1)}, u32[]{:S(2)}, u32[]{:S(2)}) collective-permute-start(bf16[128,4096]{1,0:T(8,128)(2,1)S(1)} %fusion.11), channel_id=1, source_target_pairs={{8,0},{16,8},{24,16},{32,24},{40,32},{48,40},{56,48},{64,56},{72,6... | collective-permute-start | bytes 3145736 | tf_op jit(solution)/shard_map/ppermute | solution.py:27
  224.1 17.5 %collective-permute-start = (bf16[128,4096]{1,0:T(8,128)(2,1)S(1)}, bf16[128,4096]{1,0:T(8,128)(2,1)S(1)}, u32[]{:S(2)}, u32[]{:S(2)}) collective-permute-start(bf16[128,4096]{1,0:T(8,128)(2,1)S(1)} %fusion.3), channel_id=1, source_target_pairs={{0,8},{8,16},{16,24},{24,32},{32,40},{40,48},{48,56},{56,64},{64,7... | collective-permute-start | bytes 3145736 | tf_op jit(solution)/shard_map/ppermute | solution.py:27

commit v4 on v3

--- a/solution.py
+++ b/solution.py
@@ -2,6 +2,7 @@
 
 import jax
 import jax.numpy as jnp
+import numpy as np
 from jax import lax
 from jax.experimental import pallas as pl
 from jax.experimental.pallas import tpu as pltpu
@@ -21,17 +22,14 @@
 rope_base = 500000.0
 
 
-def passed_along(shard, axis, by):
-    peers = lax.axis_size(axis)
-    pairs = [(i, i + by) for i in range(peers) if 0 <= i + by < peers]
-    return lax.ppermute(shard, axis, pairs)
-
-
-def rotation_tables(positions):
+def rotation_tables():
     half = HEAD_SIZE // 2
-    freqs = rope_base ** (-(jnp.arange(half, dtype=jnp.float32) * 2.0 / HEAD_SIZE))
-    angles = positions[:, None] * freqs[None, :]
-    return (jnp.cos(angles), jnp.sin(angles))
+    freqs = rope_base ** (-(np.arange(half) * 2.0 / HEAD_SIZE))
+    angles = np.arange(8 * ROWS)[:, None] * freqs[None, :]
+    cosines, sines = np.cos(angles), np.sin(angles)
+    cos_wide = np.concatenate([cosines, cosines], 1).astype(np.float32)
+    sin_wide = np.concatenate([-sines, sines], 1).astype(np.float32)
+    return (cos_wide, sin_wide, cos_wide.T.copy(), sin_wide.T.copy())
 
 
 def window(block):
@@ -44,7 +42,7 @@
     shape = (count, 256)
     keys = begin + lax.broadcasted_iota(jnp.int32, shape, 0)
     queries = block * 256 + lax.broadcasted_iota(jnp.int32, shape, 1)
-    same = docs_col[pl.ds(begin, count), :] == docs_row[:, pl.ds(block * 256, 256)]
+    same = docs_col[pl.ds(begin, count), 0:1] == docs_row[:, pl.ds(block * 256, 256)]
     bias[pl.ds(0, count), :] = jnp.where((keys <= queries) & same, 0.0, -1e30)
 
 
@@ -123,6 +121,35 @@
     return lax.rsqrt(jnp.mean(hidden * hidden, axis=-1, keepdims=True) + epsilon)
 
 
+def norm_rows(hidden_ref, gain_ref, whole, first_row):
+    @pl.loop(0, ROWS // 16)
+    def _(step):
+        hidden = hidden_ref[pl.ds(pl.multiple_of(step * 16, 16), 16), :].astype(jnp.float32)
+        normed = (hidden * token_scale(hidden) * gain_ref[...]).astype(jnp.bfloat16)
+        whole[pl.ds(pl.multiple_of(first_row + step * 16, 16), 16), :] = normed
+
+
+def residual_rows(hidden_ref, owned):
+    @pl.loop(0, ROWS // 16)
+    def _(step):
+        rows = pl.ds(pl.multiple_of(step * 16, 16), 16)
+        owned[rows, :] = (
+            hidden_ref[rows, :].astype(jnp.float32) + owned[rows, :].astype(jnp.float32)
+        ).astype(jnp.bfloat16)
+
+
+def gradient_rows(piece, hidden_ref, grad_rows, gain_ref, sum_ref, out):
+    @pl.loop(0, 2)
+    def _(step):
+        rows = pl.ds(pl.multiple_of(piece * 32 + step * 16, 16), 16)
+        hidden = hidden_ref[rows, :].astype(jnp.float32)
+        scale = token_scale(hidden)
+        gained = gain_ref[...] * sum_ref[rows, :]
+        inner_sum = jnp.sum(hidden * gained, axis=-1, keepdims=True)
+        norm_part = scale * gained - hidden * (scale * scale * scale * inner_sum / MODEL_WIDTH)
+        out[rows, :] = (grad_rows[rows, :].astype(jnp.float32) + norm_part).astype(jnp.bfloat16)
+
+
 def place():
     me = lax.axis_index("seq")
     return me, me // 2, me % 2
@@ -143,7 +170,7 @@
             dst_ref=dst,
             send_sem=self.send_sems.at[self.base + number],
             recv_sem=self.recv_sems.at[self.base + number],
-            device_id={"seq": peer},
+            device_id=peer if isinstance(peer, dict) else {"seq": peer},
             device_id_type=MESH,
         )
 
@@ -163,8 +190,9 @@
 def greet(peers):
     barrier = pltpu.get_barrier_semaphore()
     for peer in peers:
-        pl.semaphore_signal(barrier, inc=1, device_id={"seq": peer}, device_id_type=MESH)
-    pl.semaphore_wait(barrier, len(peers))
+        device = peer if isinstance(peer, dict) else {"seq": peer}
+        pl.semaphore_signal(barrier, inc=1, device_id=device, device_id_type=MESH)
+    return barrier
 
 
 def load_weights(weight_refs, whole_weight, sems):
@@ -200,7 +228,7 @@
         )
 
 
-def gather_steps(copies, own, whole):
+def gather_steps(copies, whole):
     me, x, z = place()
     right, left, partner = peer_of(x + 1, z), peer_of(x + 3, z), peer_of(x, 1 - z)
 
@@ -209,7 +237,7 @@
         return whole.at[pl.ds(start, count), :]
 
     def own_part(offset, count):
-        return own.at[pl.ds(offset, count), :]
+        return part(x, z, offset, count)
 
     def send(number, peer, xx, zz, offset, count):
         copies.send(number, part(xx, zz, offset, count), part(xx, zz, offset, count), peer)
@@ -299,22 +327,33 @@
 
 
 def tick_kernel(
-    own_back,
-    own_forward,
-    grad_ref,
+    back_hbm,
+    forward_hbm,
+    grad_hbm,
     query_ref,
     key_ref,
     value_ref,
+    cos_hbm,
+    sin_hbm,
+    cos_turned_hbm,
+    sin_turned_hbm,
+    gain_ref,
+    back_docs,
+    forward_docs,
+    section_out,
+    gradient_out,
+    back_hidden,
+    forward_hidden,
+    grad_ref,
     cos_ref,
     sin_ref,
     cos_turned,
     sin_turned,
     back_col,
-    back_row,
     forward_col,
-    forward_row,
     sum_ref,
     owned_ref,
+    gradient,
     whole_back,
     whole_forward,
     weight,
@@ -345,7 +384,15 @@
 ):
     me, x, z = place()
     right, left, partner = peer_of(x + 1, z), peer_of(x + 3, z), peer_of(x, 1 - z)
-    loads = load_weights((query_ref, key_ref, value_ref), weight, local_sems)
+    section = lax.axis_index("section")
+    after, before = (section + 1) % 16, (section + 15) % 16
+    first_load = pltpu.make_async_copy(back_hbm, back_hidden, local_sems.at[7])
+    first_load.start()
+    others = [(me + step) % 8 for step in range(1, 8)]
+    sources = [(me + 8 - step) % 8 for step in range(1, 8)]
+    barrier = greet([*others, {"section": after}, {"section": before}])
+    back_row = back_docs[pl.ds(section, 1), :].astype(jnp.float32)
+    forward_row = forward_docs[pl.ds(section, 1), :].astype(jnp.float32)
 
     def wide_rows(ref, peer):
         return ref.at[pl.ds(pl.multiple_of(peer * ROWS, ROWS), ROWS), :]
@@ -353,35 +400,47 @@
     def wide_cols(ref, peer):
         return ref.at[:, pl.ds(pl.multiple_of(peer * HEADS_WIDE, HEADS_WIDE), HEADS_WIDE)]
 
+    pairs = [
+        (wide_cols(grad_hbm, me), wide_rows(back_grads, me)),
+        (cos_hbm, cos_ref),
+        (sin_hbm, sin_ref),
+        (forward_hbm, forward_hidden),
+        (cos_turned_hbm, cos_turned),
+        (sin_turned_hbm, sin_turned),
+        (grad_hbm, grad_ref),
+    ]
     kept = [
-        pltpu.make_async_copy(own_back, wide_rows(whole_back, me), local_sems.at[3]),
-        pltpu.make_async_copy(own_forward, wide_rows(whole_forward, me), local_sems.at[4]),
-        pltpu.make_async_copy(wide_cols(grad_ref, me), wide_rows(back_grads, me), local_sems.at[5]),
+        pltpu.make_async_copy(src, dst, local_sems.at[8 + i]) for i, (src, dst) in enumerate(pairs)
     ]
+    first_load.wait()
+    loads = load_weights((query_ref, key_ref, value_ref), weight, local_sems)
     for one in kept:
         one.start()
-    others = [(me + step) % 8 for step in range(1, 8)]
-    sources = [(me + 8 - step) % 8 for step in range(1, 8)]
-    greet(others)
+    norm_rows(back_hidden, gain_ref, whole_back, me * ROWS)
+    pl.semaphore_wait(barrier, 9)
     back_copies = Copies(send_sems, recv_sems, 0)
     forward_copies = Copies(send_sems, recv_sems, 18)
     grad_copies = Copies(send_sems, recv_sems, 36)
     mixed_copies = Copies(send_sems, recv_sems, 43)
     copies = Copies(send_sems, recv_sems, 50)
-    back = gather_steps(back_copies, own_back, whole_back)
-    forward = gather_steps(forward_copies, own_forward, whole_forward)
+    section_copies = Copies(send_sems, recv_sems, 67)
+    back = gather_steps(back_copies, whole_back)
+    forward = gather_steps(forward_copies, whole_forward)
 
     def project(pair, whole, out):
         project_rows(pair % 4, whole, weight, cos_ref, sin_ref, out)
 
     back.begin()
+    for one in loads + kept:
+        one.wait()
+    norm_rows(forward_hidden, gain_ref, whole_forward, me * ROWS)
+    back_col[...] = jnp.broadcast_to(back_row, (128, 1024)).T
+    forward_col[...] = jnp.broadcast_to(forward_row, (128, 1024)).T
     back.relay_partner()
     back.relay_high()
     back.relay_low()
     for number, peer in enumerate(others):
         grad_copies.send(number, wide_cols(grad_ref, peer), wide_rows(back_grads, me), peer)
-    for one in loads + kept:
-        one.wait()
     back.own_pair()
     project(x, whole_back, back_heads)
     back.relay_partner_low()
@@ -538,10 +597,57 @@
     kept_mixed.wait()
     for number, peer in enumerate(sources):
         mixed_copies.arrived(number, wide_cols(owned_ref, peer), peer)
+    residual_rows(forward_hidden, owned_ref)
+
+    def piece_rows(ref, piece):
+        return ref.at[pl.ds(piece * 32, 32), :]
+
+    forward_out = section_copies.copy(0, owned_ref, section_out, {"section": after})
+
+    def gradient_copy(piece, src):
+        return section_copies.copy(
+            1 + piece, piece_rows(src, piece), piece_rows(gradient_out, piece), {"section": before}
+        )
+
+    def send_piece(piece):
+        @pl.when(section > 0)
+        def _():
+            gradient_copy(piece, gradient).start()
+
+    @pl.when(section < 15)
+    def _():
+        forward_out.start()
+
     copies.arrived(4, z_last, partner)
     total([share(x, z, 2048, 2048), near_right.at[z], near_left.at[z], z_last], 2048)
+    for piece in range(4):
+        gradient_rows(piece, back_hidden, grad_ref, gain_ref, sum_ref, gradient)
+        if piece > 0:
+            send_piece(piece - 1)
+    send_piece(3)
+
+    @pl.when(section == 0)
+    def _():
+        section_out[...] = jnp.zeros_like(section_out)
+
+    @pl.when(section == 15)
+    def _():
+        gradient_out[...] = jnp.zeros_like(gradient_out)
+
     for each in (back_copies, forward_copies, grad_copies, mixed_copies, copies):
         each.finish()
+
+    @pl.when(section < 15)
+    def _():
+        forward_out.wait_send()
+        for piece in range(4):
+            gradient_copy(piece, gradient_out).wait_recv()
+
+    @pl.when(section > 0)
+    def _():
+        section_copies.copy(0, section_out, section_out, {"section": before}).wait_recv()
+        for piece in range(4):
+            gradient_copy(piece, gradient).wait_send()
 
 
 def tick(operands, weights):
@@ -549,17 +655,28 @@
     anywhere = pl.BlockSpec(memory_space=pl.ANY)
     bf16, f32 = jnp.bfloat16, jnp.float32
     all_operands = [*operands[:3], *weights, *operands[3:]]
-    in_specs = [vmem] * len(all_operands)
-    in_specs[3:6] = [anywhere] * 3
+    in_specs = [anywhere] * 10 + [vmem] * 3
     return pl.pallas_call(
         tick_kernel,
         out_shape=[
-            jax.ShapeDtypeStruct((ROWS, COLS), f32),
+            jax.ShapeDtypeStruct((ROWS, COLS), bf16),
             jax.ShapeDtypeStruct((ROWS, COLS), bf16),
         ],
         in_specs=in_specs,
         out_specs=[vmem, vmem],
         scratch_shapes=[
+            pltpu.VMEM((ROWS, COLS), bf16),
+            pltpu.VMEM((ROWS, COLS), bf16),
+            pltpu.VMEM((ROWS, COLS), bf16),
+            pltpu.VMEM((1024, HEAD_SIZE), f32),
+            pltpu.VMEM((1024, HEAD_SIZE), f32),
+            pltpu.VMEM((HEAD_SIZE, 1024), f32),
+            pltpu.VMEM((HEAD_SIZE, 1024), f32),
+            pltpu.VMEM((1024, 128), f32),
+            pltpu.VMEM((1024, 128), f32),
+            pltpu.VMEM((ROWS, COLS), f32),
+            pltpu.VMEM((ROWS, COLS), bf16),
+            pltpu.VMEM((ROWS, COLS), bf16),
             pltpu.VMEM((1024, COLS), bf16),
             pltpu.VMEM((1024, COLS), bf16),
             pltpu.VMEM((COLS, ALL_WIDE), bf16),
@@ -584,9 +701,9 @@
             pltpu.VMEM((2048, ROWS), bf16),
             pltpu.VMEM((2048, ROWS), bf16),
             pltpu.VMEM((2048, ROWS), bf16),
-            pltpu.SemaphoreType.DMA((7,)),
-            pltpu.SemaphoreType.DMA((67,)),
-            pltpu.SemaphoreType.DMA((67,)),
+            pltpu.SemaphoreType.DMA((15,)),
+            pltpu.SemaphoreType.DMA((72,)),
+            pltpu.SemaphoreType.DMA((72,)),
         ],
         compiler_params=pltpu.CompilerParams(
             collective_id=0, has_side_effects=True, vmem_limit_bytes=66000000
@@ -605,45 +722,18 @@
     key_matrix,
     value_matrix,
 ):
-    section_index = lax.axis_index("section")
-    first_docs = lax.dynamic_index_in_dim(forward_docs, section_index, 0, keepdims=False)
-    back_docs = lax.dynamic_index_in_dim(backward_docs, section_index, 0, keepdims=False)
-    gain_row = norm_gain[0]
-    weights = (query_weight[0], key_matrix[0], value_matrix[0])
-    forward_hidden = forward_rows[0].astype(jnp.float32)
-    forward_normed = (forward_hidden * token_scale(forward_hidden) * gain_row).astype(jnp.bfloat16)
-    back_hidden = saved_rows[0].astype(jnp.float32)
-    back_scale = token_scale(back_hidden)
-    back_normed = (back_hidden * back_scale * gain_row).astype(jnp.bfloat16)
-    cosines, sines = rotation_tables(jnp.arange(8 * ROWS, dtype=jnp.float32))
-    cos_wide = jnp.concatenate([cosines, cosines], 1)
-    sin_wide = jnp.concatenate([-sines, sines], 1)
-    input_sum, owned_rows = tick(
+    section_output, input_grad = tick(
         (
-            back_normed,
-            forward_normed,
+            saved_rows[0],
+            forward_rows[0],
             output_grad[0],
-            cos_wide,
-            sin_wide,
-            cos_wide.T,
-            sin_wide.T,
-            back_docs[:, None],
-            back_docs[None, :],
-            first_docs[:, None],
-            first_docs[None, :],
+            *(jnp.asarray(table) for table in rotation_tables()),
+            norm_gain,
+            backward_docs,
+            forward_docs,
         ),
-        weights,
+        (query_weight[0], key_matrix[0], value_matrix[0]),
     )
-    first_out = (forward_hidden + owned_rows.astype(jnp.float32)).astype(jnp.bfloat16)
-    section_output = passed_along(first_out, "section", 1)
-    gained = gain_row * input_sum
-    inner_sum = jnp.sum(back_hidden * gained, axis=-1, keepdims=True)
-    norm_part = (
-        back_scale * gained
-        - back_hidden * (back_scale * back_scale * back_scale) * inner_sum / MODEL_WIDTH
-    )
-    first_grad = (output_grad[0].astype(jnp.float32) + norm_part).astype(jnp.bfloat16)
-    input_grad = passed_along(first_grad, "section", -1)
     return (section_output[None], input_grad[None])
 
 

time: 246 us -> 223 us (0.907)
  Pallas kernels: 202 us -> 218 us
  other arithmetic: 12.1 us -> 0 us
  waiting for transfers between devices: 11.7 us -> 0 us
  starting transfers between devices: 9.18 us -> 0 us
  local copies, waits for them, and re-layouts: 7.33 us -> 4.57 us
    pallas_call x1, Pallas kernels: 202 us -> 218 us  [tick(): pl.pallas_call(tick_kernel, out_shape=[jax.ShapeDtypeStruct((ROWS, COLS),...]
    ppermute x2 -> x0, waiting for transfers between devices: 11.7 us -> none  [passed_along(): return lax.ppermute(shard, axis, pairs)]
    ppermute x2 -> x0, starting transfers between devices: 9.18 us -> none  [passed_along(): return lax.ppermute(shard, axis, pairs)]
    reduce_sum x3 -> x0, other arithmetic: 5.4 us -> none  [the longest x2 3.04 us: token_scale(): jnp.mean(hidden * hidden, axis=-1, keepdims=True) + epsilon]
    convert_element_type x3 -> x0, other arithmetic: 4.44 us -> none  [the longest x1 2.22 us: body(): (output_grad[0].astype(jnp.float32) + norm_part).astype(jnp.bfloat16)]
  transfers between devices with their start and end apart: 2 -> 0, of which waited for: 2 -> 0; matrix products, arithmetic and copies ran while one was open for 0% -> 0% of each run, Pallas kernels for 0% -> 0%
where the time goes in v4:
time: 223 us
  Pallas kernels  218 us (98%)
  local copies, waits for them, and re-layouts  4.57 us (2%)
    pallas_call x1, Pallas kernels, tick(): pl.pallas_call(tick_kernel, out_shape=[jax.ShapeDtypeStruct((ROWS, COLS),...  218 us
    unnamed x2, local copies, waits for them, and re-layouts  4.57 us

profile of v4, /device:TPU:25, one launch (start us, length us, event | category | flops | bytes accessed | tf_op | source)
XLA Modules:
  0.0 222.9 jit_solution(13403691016460266155)
XLA Ops:
  0.6 217.7 %shard_map.140 = (bf16[128,4096]{1,0:T(8,128)(2,1)}, bf16[128,4096]{1,0:T(8,128)(2,1)}) custom-call(bf16[128,4096]{1,0:T(8,128)(2,1)} %bitcast.9, bf16[128,4096]{1,0:T(8,128)(2,1)} %bitcast.10, bf16[128,4096]{1,0:T(8,128)(2,1)} %bitcast.11, bf16[4096,512]{1,0:T(8,128)(2,1)} %bitcast.8, bf16[4096,128]{1,0:T(8,128)(2,1)} %bitcast.12, ...), custom_call_target="tpu_custom_call" | custom-call | tf_op jit(solution)/shard_map/pallas_call | solution.py:659
  218.3 2.3 %copy.17 = bf16[1,128,4096]{2,1,0:T(8,128)(2,1)} copy(bf16[1,128,4096]{2,1,0:T(8,128)(2,1)} %bitcast.15) | data formatting | bytes 2097152
  220.6 2.3 %copy.18 = bf16[1,128,4096]{2,1,0:T(8,128)(2,1)} copy(bf16[1,128,4096]{2,1,0:T(8,128)(2,1)} %bitcast.14) | data formatting | bytes 2097152

commit v5 on v4

--- a/solution.py
+++ b/solution.py
@@ -129,12 +129,14 @@
         whole[pl.ds(pl.multiple_of(first_row + step * 16, 16), 16), :] = normed
 
 
-def residual_rows(hidden_ref, owned):
-    @pl.loop(0, ROWS // 16)
+def residual_cols(hidden_ref, owned, peer):
+    cols = pl.ds(pl.multiple_of(peer * HEADS_WIDE, HEADS_WIDE), HEADS_WIDE)
+
+    @pl.loop(0, 2)
     def _(step):
-        rows = pl.ds(pl.multiple_of(step * 16, 16), 16)
-        owned[rows, :] = (
-            hidden_ref[rows, :].astype(jnp.float32) + owned[rows, :].astype(jnp.float32)
+        rows = pl.ds(pl.multiple_of(step * 64, 64), 64)
+        owned[rows, cols] = (
+            hidden_ref[rows, cols].astype(jnp.float32) + owned[rows, cols].astype(jnp.float32)
         ).astype(jnp.bfloat16)
 
 
@@ -557,12 +559,13 @@
     add_rows(spot, [spot, z_in.at[3, pl.ds(0, 1024), :]], 1024)
     copies.send(15, spot, near_left_one.at[pl.ds(0, 1024), :], left)
     attend(3)
-    kept_mixed = pltpu.make_async_copy(
-        wide_rows(mixed_ref, me), wide_cols(owned_ref, me), local_sems.at[6]
-    )
-    kept_mixed.start()
-    for number, peer in enumerate(others):
-        mixed_copies.send(number, wide_rows(mixed_ref, peer), wide_cols(owned_ref, me), peer)
+    copies.arrived(6, near_right.at[:, pl.ds(1024, 1024), :], left)
+    copies.arrived(12, near_left.at[:, pl.ds(0, 1024), :], right)
+    copies.arrived(7, near_right.at[:, pl.ds(0, 1024), :], left)
+    copies.arrived(13, near_left.at[:, pl.ds(1024, 1024), :], right)
+    spot = share(x, 1 - z, 2048, 2048)
+    add_rows(spot, [spot, near_right.at[1 - z], near_left.at[1 - z]], 2048)
+    copies.send(4, spot, z_last, partner)
     copies.arrived(8, far_right_one, left)
     spot = share(x + 1, z, 0, 1024)
     add_rows(spot, [spot, z_in.at[1, pl.ds(0, 1024), :], far_right_one], 1024)
@@ -571,13 +574,12 @@
     spot = share(x + 3, z, 1024, 1024)
     add_rows(spot, [spot, z_in.at[3, pl.ds(1024, 1024), :], far_left_one], 1024)
     copies.send(16, spot, near_left_one.at[pl.ds(1024, 1024), :], left)
-    copies.arrived(6, near_right.at[:, pl.ds(1024, 1024), :], left)
-    copies.arrived(12, near_left.at[:, pl.ds(0, 1024), :], right)
-    copies.arrived(7, near_right.at[:, pl.ds(0, 1024), :], left)
-    copies.arrived(13, near_left.at[:, pl.ds(1024, 1024), :], right)
-    spot = share(x, 1 - z, 2048, 2048)
-    add_rows(spot, [spot, near_right.at[1 - z], near_left.at[1 - z]], 2048)
-    copies.send(4, spot, z_last, partner)
+    kept_mixed = pltpu.make_async_copy(
+        wide_rows(mixed_ref, me), wide_cols(owned_ref, me), local_sems.at[6]
+    )
+    kept_mixed.start()
+    for number, peer in enumerate(others):
+        mixed_copies.send(number, wide_rows(mixed_ref, peer), wide_cols(owned_ref, me), peer)
 
     def total(terms, offset):
         @pl.loop(0, 8)
@@ -594,29 +596,19 @@
     copies.arrived(10, near_right_one.at[pl.ds(0, 1024), :], left)
     copies.arrived(16, near_left_one.at[pl.ds(1024, 1024), :], right)
     total([share(x, z, 0, 2048), z_in.at[0], near_right_one, near_left_one], 0)
-    kept_mixed.wait()
-    for number, peer in enumerate(sources):
-        mixed_copies.arrived(number, wide_cols(owned_ref, peer), peer)
-    residual_rows(forward_hidden, owned_ref)
 
     def piece_rows(ref, piece):
         return ref.at[pl.ds(piece * 32, 32), :]
 
-    forward_out = section_copies.copy(0, owned_ref, section_out, {"section": after})
-
     def gradient_copy(piece, src):
         return section_copies.copy(
-            1 + piece, piece_rows(src, piece), piece_rows(gradient_out, piece), {"section": before}
+            8 + piece, piece_rows(src, piece), piece_rows(gradient_out, piece), {"section": before}
         )
 
     def send_piece(piece):
         @pl.when(section > 0)
         def _():
             gradient_copy(piece, gradient).start()
-
-    @pl.when(section < 15)
-    def _():
-        forward_out.start()
 
     copies.arrived(4, z_last, partner)
     total([share(x, z, 2048, 2048), near_right.at[z], near_left.at[z], z_last], 2048)
@@ -626,6 +618,25 @@
             send_piece(piece - 1)
     send_piece(3)
 
+    def forward_copy(number, peer, src, to):
+        return section_copies.copy(
+            number, wide_cols(src, peer), wide_cols(section_out, peer), {"section": to}
+        )
+
+    def start_forward(number, peer):
+        @pl.when(section < 15)
+        def _():
+            forward_copy(number, peer, owned_ref, after).start()
+
+    for number, peer in enumerate([me, *sources]):
+        if number == 0:
+            kept_mixed.wait()
+        else:
+            mixed_copies.arrived(number - 1, wide_cols(owned_ref, peer), peer)
+        residual_cols(forward_hidden, owned_ref, peer)
+        if number > 0:
+            start_forward(number - 1, [me, *sources][number - 1])
+
     @pl.when(section == 0)
     def _():
         section_out[...] = jnp.zeros_like(section_out)
@@ -634,18 +645,21 @@
     def _():
         gradient_out[...] = jnp.zeros_like(gradient_out)
 
+    start_forward(7, sources[6])
     for each in (back_copies, forward_copies, grad_copies, mixed_copies, copies):
         each.finish()
 
     @pl.when(section < 15)
     def _():
-        forward_out.wait_send()
+        for number, peer in enumerate([me, *sources]):
+            forward_copy(number, peer, owned_ref, after).wait_send()
         for piece in range(4):
             gradient_copy(piece, gradient_out).wait_recv()
 
     @pl.when(section > 0)
     def _():
-        section_copies.copy(0, section_out, section_out, {"section": before}).wait_recv()
+        for number, peer in enumerate([me, *sources]):
+            forward_copy(number, peer, section_out, before).wait_recv()
         for piece in range(4):
             gradient_copy(piece, gradient).wait_send()
 
@@ -702,8 +716,8 @@
             pltpu.VMEM((2048, ROWS), bf16),
             pltpu.VMEM((2048, ROWS), bf16),
             pltpu.SemaphoreType.DMA((15,)),
-            pltpu.SemaphoreType.DMA((72,)),
-            pltpu.SemaphoreType.DMA((72,)),
+            pltpu.SemaphoreType.DMA((79,)),
+            pltpu.SemaphoreType.DMA((79,)),
         ],
         compiler_params=pltpu.CompilerParams(
             collective_id=0, has_side_effects=True, vmem_limit_bytes=66000000

time: 223 us -> 222 us (level)
  no operation moved by 1% of the time
where the time goes in v5:
time: 222 us; the launch traced here: 221 us
  Pallas kernels  216 us (97%)
  local copies, waits for them, and re-layouts  4.57 us (2%)
    pallas_call x1, Pallas kernels, tick(): pl.pallas_call(tick_kernel, out_shape=[jax.ShapeDtypeStruct((ROWS, COLS),...  216 us
    unnamed x2, local copies, waits for them, and re-layouts  4.57 us

profile of v5, /device:TPU:25, one launch (start us, length us, event | category | flops | bytes accessed | tf_op | source)
XLA Modules:
  0.0 221.3 jit_solution(9365952580930550978)
XLA Ops:
  0.6 216.1 %shard_map.140 = (bf16[128,4096]{1,0:T(8,128)(2,1)}, bf16[128,4096]{1,0:T(8,128)(2,1)}) custom-call(bf16[128,4096]{1,0:T(8,128)(2,1)} %bitcast.9, bf16[128,4096]{1,0:T(8,128)(2,1)} %bitcast.10, bf16[128,4096]{1,0:T(8,128)(2,1)} %bitcast.11, bf16[4096,512]{1,0:T(8,128)(2,1)} %bitcast.8, bf16[4096,128]{1,0:T(8,128)(2,1)} %bitcast.12, ...), custom_call_target="tpu_custom_call" | custom-call | tf_op jit(solution)/shard_map/pallas_call | solution.py:673
  216.8 2.3 %copy.17 = bf16[1,128,4096]{2,1,0:T(8,128)(2,1)} copy(bf16[1,128,4096]{2,1,0:T(8,128)(2,1)} %bitcast.15) | data formatting | bytes 2097152
  219.1 2.3 %copy.18 = bf16[1,128,4096]{2,1,0:T(8,128)(2,1)} copy(bf16[1,128,4096]{2,1,0:T(8,128)(2,1)} %bitcast.14) | data formatting | bytes 2097152

commit v6 on v5

--- a/solution.py
+++ b/solution.py
@@ -748,7 +748,12 @@
         ),
         (query_weight[0], key_matrix[0], value_matrix[0]),
     )
-    return (section_output[None], input_grad[None])
+    section = lax.axis_index("section")
+    zero = jnp.zeros((), jnp.bfloat16)
+    return (
+        jnp.where(section == 0, zero, section_output)[None],
+        jnp.where(section == 15, zero, input_grad)[None],
+    )
 
 
 def solution(mesh):

time: 222 us -> 220 us (level)
  local copies, waits for them, and re-layouts: 4.57 us -> 0 us
  other arithmetic: 0 us -> 3.01 us
    unnamed x2 -> x0, local copies, waits for them, and re-layouts: 4.57 us -> none
    broadcast_in_dim x0 -> x1, other arithmetic: none -> 3.01 us  [body(): jnp.where(section == 15, zero, input_grad)[None]]
where the time goes in v6:
time: 220 us
  Pallas kernels  216 us (98%)
  other arithmetic  3.01 us (1%)
    pallas_call x1, Pallas kernels, tick(): pl.pallas_call(tick_kernel, out_shape=[jax.ShapeDtypeStruct((ROWS, COLS),...  216 us

profile of v6, /device:TPU:25, one launch (start us, length us, event | category | flops | bytes accessed | tf_op | source)
XLA Modules:
  0.0 219.8 jit_solution(12306891376599621)
XLA Ops:
  0.6 216.1 %shard_map.140 = (bf16[128,4096]{1,0:T(8,128)(2,1)}, bf16[128,4096]{1,0:T(8,128)(2,1)}) custom-call(bf16[128,4096]{1,0:T(8,128)(2,1)} %bitcast.11, bf16[128,4096]{1,0:T(8,128)(2,1)} %bitcast.12, bf16[128,4096]{1,0:T(8,128)(2,1)} %bitcast.13, bf16[4096,512]{1,0:T(8,128)(2,1)} %bitcast.10, bf16[4096,128]{1,0:T(8,128)(2,1)} %bitcast.14, ...), custom_call_target="tpu_custom_call" | custom-call | tf_op jit(solution)/shard_map/pallas_call | solution.py:673
  216.8 3.0 %select_bitcast_fusion = (bf16[1,128,4096]{2,1,0:T(8,128)(2,1)}, bf16[1,128,4096]{2,1,0:T(8,128)(2,1)}) fusion(bf16[128,4096]{1,0:T(8,128)(2,1)} %get-tuple-element.5, pred[]{:T(512)S(6)} %eq.7, bf16[128,4096]{1,0:T(8,128)(2,1)} %get-tuple-element.4, pred[]{:T(512)S(6)} %eq.6), kind=kLoop, calls=%fused_computation | loop fusion | flops 1048576 | bytes 4194306 | tf_op jit(solution)/shard_map/broadcast_in_dim | solution.py:755
